TPU v7x, 32 devices: a whole 2x2x4 slice. The times are simulated.
32 devices in a mesh: groups: 2 (over y), pairs: 8 (over z, x), rows: 2 (over core).
Axes of the slice: x: 2, y: 2, z: 4, core: 2. Of those that a mesh axis runs over, the one named last changes fastest.
Arguments:
- first_image: float32 [16, 128, 256], P(('groups', 'pairs'), 'rows'), parts along dimension 0, may hold values from -12 to 12
- second_image: float32 [16, 128, 256], P(('groups', 'pairs'), 'rows'), parts along dimension 0, may hold values from -12 to 12
- prior_motion: float32 [2, 16, 128, 256], P(None, ('groups', 'pairs'), 'rows'), parts along dimension 1, may hold values from -40 to 40
- offsets: int32 [64, 2], replicated, may hold values from -4 to 4, as said below
- pair_epochs: int32 [16, 2], P('groups'), parts along dimension 0, may hold values from 0 to 128, as said below
- pair_slot: int32 [16], P('groups'), parts along dimension 0, may hold values from 0 to 7, each once
Outputs:
- velocity: float32 [2, 128, 4, 16384], P(None, None, ('groups', 'rows'), 'pairs'), parts along dimension 2
- motion: float32 [2, 16, 128, 256], P(None, ('groups', 'pairs'), 'rows'), parts along dimension 1
There are 2 independent parts, one for each index of `groups`. A program takes and returns all parts, laid end to end along the dimension named above; an argument that names none is the same for every part. Nothing has to cross between parts.
Inputs may be any that keep to these rules, and one draw needn't show every extreme that they name: 64 distinct offsets; every offset with a component of magnitude 4 is among them. `pair_epochs`: each row has first < after. `pair_slot`: a permutation of the pairs.
All inputs are finite; a program needn't handle non-finite values. Where the computation divides by a largest or mean magnitude, that divisor is 1e-20 or more.
Results may differ from a plain program's by a relative error of at most 0.0003.
Values sent between devices are 32-bit elements; how exact they have to be, the bound alone decides.
No kernel may reach another device: no remote copies, remote signals or barrier semaphores. Data moves between devices by JAX's collectives and lax.ppermute only.
A program may use at most 64 MiB of HBM per device.

v0:
```python
import jax
import jax.numpy as jnp
from jax import lax
from jax.sharding import PartitionSpec as P

OFFSETS = 64
SEARCH = 4
RADIUS = 4
EPOCHS = 128
ITERS = 4
ROUNDS = 2


SOFTMIN_HEAT = 0.1
PRIOR_STRENGTH = 0.05
PENALTY = 4.0
SPARSITY = 0.4
VARIANCE_FLOOR = 0.05
HIGHEST = lax.Precision.HIGHEST
NEWTON_STEPS = 32


def with_halo(cells, sides, width):
    for axis, dim in sides:
        count = lax.axis_size(axis)
        ends = count - 1
        head = lax.slice_in_dim(cells, 0, width, axis=dim)
        tail = lax.slice_in_dim(cells, cells.shape[dim] - width, cells.shape[dim], axis=dim)
        cells = jnp.concatenate(
            [
                lax.ppermute(tail, axis, [(i, (i + 1) % count) for i in range(ends)]),
                cells,
                lax.ppermute(head, axis, [((i + 1) % count, i) for i in range(ends)]),
            ],
            axis=dim,
        )
    return cells


def invert_normal(normal_matrix):
    order = normal_matrix.shape[0]
    identity = jnp.eye(order, dtype=jnp.float32)
    column_bound = jnp.max(jnp.sum(jnp.abs(normal_matrix), axis=0))
    estimate = identity / column_bound
    for step in range(NEWTON_STEPS):
        product = jnp.dot(normal_matrix, estimate, precision=HIGHEST)
        estimate = jnp.dot(estimate, 2.0 * identity - product, precision=HIGHEST)
    return estimate


def box_sum(values):
    window = 2 * RADIUS + 1
    height = values.shape[-2] - 2 * RADIUS
    breadth = values.shape[-1] - 2 * RADIUS
    running = values[..., 0:height, :]
    for position in range(1, window):
        running = running + values[..., position : position + height, :]
    summed = running[..., 0:breadth]
    for position in range(1, window):
        summed = summed + running[..., position : position + breadth]
    return summed / float(window * window)


def correlate(
    shift_vector,
    first_padded,
    second_padded,
    mean_first,
    var_first,
    mean_second_all,
    square_second_all,
    height,
    columns,
):
    row_start = shift_vector[0] + SEARCH
    col_start = shift_vector[1] + SEARCH
    mean_second = lax.dynamic_slice(mean_second_all, (row_start, col_start), (height, columns))
    square_second = lax.dynamic_slice(square_second_all, (row_start, col_start), (height, columns))
    window_second = lax.dynamic_slice(
        second_padded, (row_start, col_start), (height + 2 * RADIUS, columns + 2 * RADIUS)
    )
    covariance = box_sum(first_padded * window_second) - mean_first * mean_second
    var_second = square_second - mean_second * mean_second
    return covariance / jnp.sqrt(
        jnp.maximum(var_first, VARIANCE_FLOOR) * jnp.maximum(var_second, VARIANCE_FLOOR)
    )


def build_design(pair_epochs, pair_slot):
    pair_number = jnp.arange(pair_slot.shape[0], dtype=jnp.int32)
    chooser = (pair_slot[:, None] == pair_number[None, :]).astype(jnp.int32)
    starts = jnp.sum(chooser * pair_epochs[None, :, 0], axis=1)
    finishes = jnp.sum(chooser * pair_epochs[None, :, 1], axis=1)
    epoch_number = jnp.arange(EPOCHS, dtype=jnp.int32)
    inside = (epoch_number[None, :] >= starts[:, None]) & (
        epoch_number[None, :] < finishes[:, None]
    )
    return inside.astype(jnp.float32)


def per_device(first_image, second_image, prior_motion, offsets, pair_epochs, pair_slot):
    band_rows = first_image.shape[1]
    columns = first_image.shape[2]
    margin = SEARCH + RADIUS
    stacked = jnp.concatenate((first_image, second_image), axis=0)
    extended = with_halo(stacked, (("rows", 1),), margin)
    extended = jnp.pad(extended, ((0, 0), (0, 0), (margin, margin)))
    first_padded = extended[
        0, SEARCH : SEARCH + band_rows + 2 * RADIUS, SEARCH : SEARCH + columns + 2 * RADIUS
    ]
    second_padded = extended[1]
    mean_first = box_sum(first_padded)
    var_first = box_sum(first_padded * first_padded) - mean_first * mean_first
    mean_second_all = box_sum(second_padded)
    square_second_all = box_sum(second_padded * second_padded)
    offset_blocks = offsets.reshape(OFFSETS // 8, 8, 2)
    pairs_count = lax.axis_size("pairs")
    pixels = band_rows * columns // pairs_count
    design_matrix = build_design(pair_epochs, pair_slot)
    normal_matrix = jnp.dot(design_matrix.T, design_matrix, precision=HIGHEST) + PENALTY * jnp.eye(
        EPOCHS, dtype=jnp.float32
    )
    inverse_matrix = invert_normal(normal_matrix)
    threshold = SPARSITY / PENALTY
    sparse = jnp.zeros((2, EPOCHS, pixels), jnp.float32)
    scaled = jnp.zeros((2, EPOCHS, pixels), jnp.float32)
    prior_band = prior_motion[:, 0]
    motion = prior_band
    for round_number in range(ROUNDS):

        def block_step(state_now, offset_block):
            running_max, weight_sum, sum_rows, sum_cols = state_now
            cross_correlation = jax.vmap(
                lambda shift_vector: correlate(
                    shift_vector,
                    first_padded,
                    second_padded,
                    mean_first,
                    var_first,
                    mean_second_all,
                    square_second_all,
                    band_rows,
                    columns,
                )
            )(offset_block)
            shifts = offset_block.astype(jnp.float32)
            pixel_distance = (shifts[:, 0, None, None] - prior_band[0]) ** 2 + (
                shifts[:, 1, None, None] - prior_band[1]
            ) ** 2
            match_scores = (cross_correlation - PRIOR_STRENGTH * pixel_distance) / SOFTMIN_HEAT
            new_max = jnp.maximum(running_max, jnp.max(match_scores, axis=0))
            rescale = jnp.exp(running_max - new_max)
            weights = jnp.exp(match_scores - new_max)
            weight_sum = weight_sum * rescale + jnp.sum(weights, axis=0)
            sum_rows = sum_rows * rescale + jnp.sum(weights * shifts[:, 0, None, None], axis=0)
            sum_cols = sum_cols * rescale + jnp.sum(weights * shifts[:, 1, None, None], axis=0)
            return ((new_max, weight_sum, sum_rows, sum_cols), None)

        zeros_band = jnp.zeros((band_rows, columns), jnp.float32)
        initial = (
            jnp.full((band_rows, columns), -jnp.inf, jnp.float32),
            zeros_band,
            zeros_band,
            zeros_band,
        )
        (running_max, weight_sum, sum_rows, sum_cols), unused = lax.scan(
            block_step, initial, offset_blocks
        )
        motion = jnp.stack((sum_rows / weight_sum, sum_cols / weight_sum))
        outgoing = motion.reshape(2, 1, pairs_count, pixels)
        arrived = lax.all_to_all(outgoing, "pairs", split_axis=2, concat_axis=1, tiled=True)
        observed = arrived.reshape(2, arrived.shape[1], pixels)
        fixed_part = jnp.einsum("pe,cpn->cen", design_matrix, observed, precision=HIGHEST)
        for iteration in range(ITERS):
            target = fixed_part + PENALTY * (sparse - scaled)
            estimate = jnp.einsum("ef,cfn->cen", inverse_matrix, target, precision=HIGHEST)
            blended = estimate + scaled
            sparse = blended - jnp.clip(blended, -threshold, threshold)
            scaled = blended - sparse
        if round_number + 1 < ROUNDS:
            predicted = jnp.einsum("pe,cen->cpn", design_matrix, sparse, precision=HIGHEST)
            predicted = predicted.reshape(2, predicted.shape[1], 1, pixels)
            returned = lax.all_to_all(predicted, "pairs", split_axis=1, concat_axis=2, tiled=True)
            prior_band = 0.5 * (prior_motion[:, 0] + returned.reshape(2, band_rows, columns))
    return (sparse[:, :, None, :], motion[:, None])


def solution(mesh):
    placed = (
        P(("groups", "pairs"), "rows", None),
        P(("groups", "pairs"), "rows", None),
        P(None, ("groups", "pairs"), "rows", None),
        P(),
        P("groups", None),
        P("groups"),
    )
    return jax.shard_map(
        per_device,
        mesh=mesh,
        in_specs=placed,
        out_specs=(
            P(None, None, ("groups", "rows"), "pairs"),
            P(None, ("groups", "pairs"), "rows", None),
        ),
        check_vma=False,
    )
```

profile of v0, /device:TPU:0, one launch (start us, length us, event | category | flops | bytes accessed | tf_op | source)
XLA Modules:
  0.0 884.4 jit_solution(6239399067341562366)
XLA Ops:
  24.2 400.5 %while.59 = (s32[]{:T(128)}, f32[64,256]{1,0:T(8,128)S(1)}, f32[64,256]{1,0:T(8,128)S(1)}, f32[64,256]{1,0:T(8,128)S(1)}, f32[64,256]{1,0:T(8,128)S(1)}, /*index...) while((s32[]{:T(128)}, f32[64,256]{1,0:T(8,128)S(1)}, ...), condition=%wide.region_5.6_spmd.clone, body=%wide.region_0.5_spmd.clone.sunk | while | flops 5460633 | bytes 17080092 | solution.py:166
  24.3 16.0 %while.66 = (s32[]{:T(128)}, f32[80,272]{1,0:T(8,128)S(1)}, s32[8,2]{0,1:T(2,128)S(1)}, f32[8,72,264]{2,1,0:T(8,128)S(1)}, s32[]{:T(128)}) while((s32[]{:T(128)}, f32[80,272]{1,0:T(8,128)S(1)}, s32[8,2]{0,1:T(2,128)S(1)}, f32[8,72,264]{2,1,0:T(8,128)S(1)}, s32[]{:T(128)}) %tuple.266), condition=%wide.while_cond, body=%wide.while_body.sunk | while | flops 2 | bytes 221293 | solution.py:79
  41.0 15.9 %while.64 = (s32[]{:T(128)}, f32[72,264]{1,0:T(8,128)S(1)}, s32[8,2]{0,1:T(2,128)S(1)}, f32[8,64,256]{2,1,0:T(8,128)S(1)}, s32[]{:T(128)}) while((s32[]{:T(128)}, f32[72,264]{1,0:T(8,128)S(1)}, s32[8,2]{0,1:T(2,128)S(1)}, f32[8,64,256]{2,1,0:T(8,128)S(1)}, s32[]{:T(128)}) %tuple.260), condition=%wide.while_cond.2, body=%wide.while_body.2.sunk | while | flops 2 | bytes 131181 | solution.py:78
  56.9 15.9 %while.65 = (s32[]{:T(128)}, f32[72,264]{1,0:T(8,128)S(1)}, s32[8,2]{0,1:T(2,128)S(1)}, f32[8,64,256]{2,1,0:T(8,128)S(1)}, s32[]{:T(128)}) while((s32[]{:T(128)}, f32[72,264]{1,0:T(8,128)S(1)}, s32[8,2]{0,1:T(2,128)S(1)}, f32[8,64,256]{2,1,0:T(8,128)S(1)}, s32[]{:T(128)}) %tuple.282), condition=%wide.while_cond.1, body=%wide.while_body.1.sunk | while | flops 2 | bytes 131181 | solution.py:77
  74.4 16.0 %while.66 = (s32[]{:T(128)}, f32[80,272]{1,0:T(8,128)S(1)}, s32[8,2]{0,1:T(2,128)S(1)}, f32[8,72,264]{2,1,0:T(8,128)S(1)}, s32[]{:T(128)}) while((s32[]{:T(128)}, f32[80,272]{1,0:T(8,128)S(1)}, s32[8,2]{0,1:T(2,128)S(1)}, f32[8,72,264]{2,1,0:T(8,128)S(1)}, s32[]{:T(128)}) %tuple.266), condition=%wide.while_cond, body=%wide.while_body.sunk | while | flops 2 | bytes 221293 | solution.py:79
  91.1 15.9 %while.64 = (s32[]{:T(128)}, f32[72,264]{1,0:T(8,128)S(1)}, s32[8,2]{0,1:T(2,128)S(1)}, f32[8,64,256]{2,1,0:T(8,128)S(1)}, s32[]{:T(128)}) while((s32[]{:T(128)}, f32[72,264]{1,0:T(8,128)S(1)}, s32[8,2]{0,1:T(2,128)S(1)}, f32[8,64,256]{2,1,0:T(8,128)S(1)}, s32[]{:T(128)}) %tuple.260), condition=%wide.while_cond.2, body=%wide.while_body.2.sunk | while | flops 2 | bytes 131181 | solution.py:78
  107.0 15.9 %while.65 = (s32[]{:T(128)}, f32[72,264]{1,0:T(8,128)S(1)}, s32[8,2]{0,1:T(2,128)S(1)}, f32[8,64,256]{2,1,0:T(8,128)S(1)}, s32[]{:T(128)}) while((s32[]{:T(128)}, f32[72,264]{1,0:T(8,128)S(1)}, s32[8,2]{0,1:T(2,128)S(1)}, f32[8,64,256]{2,1,0:T(8,128)S(1)}, s32[]{:T(128)}) %tuple.282), condition=%wide.while_cond.1, body=%wide.while_body.1.sunk | while | flops 2 | bytes 131181 | solution.py:77
  124.4 16.0 %while.66 = (s32[]{:T(128)}, f32[80,272]{1,0:T(8,128)S(1)}, s32[8,2]{0,1:T(2,128)S(1)}, f32[8,72,264]{2,1,0:T(8,128)S(1)}, s32[]{:T(128)}) while((s32[]{:T(128)}, f32[80,272]{1,0:T(8,128)S(1)}, s32[8,2]{0,1:T(2,128)S(1)}, f32[8,72,264]{2,1,0:T(8,128)S(1)}, s32[]{:T(128)}) %tuple.266), condition=%wide.while_cond, body=%wide.while_body.sunk | while | flops 2 | bytes 221293 | solution.py:79
  141.1 15.9 %while.64 = (s32[]{:T(128)}, f32[72,264]{1,0:T(8,128)S(1)}, s32[8,2]{0,1:T(2,128)S(1)}, f32[8,64,256]{2,1,0:T(8,128)S(1)}, s32[]{:T(128)}) while((s32[]{:T(128)}, f32[72,264]{1,0:T(8,128)S(1)}, s32[8,2]{0,1:T(2,128)S(1)}, f32[8,64,256]{2,1,0:T(8,128)S(1)}, s32[]{:T(128)}) %tuple.260), condition=%wide.while_cond.2, body=%wide.while_body.2.sunk | while | flops 2 | bytes 131181 | solution.py:78
  157.1 15.9 %while.65 = (s32[]{:T(128)}, f32[72,264]{1,0:T(8,128)S(1)}, s32[8,2]{0,1:T(2,128)S(1)}, f32[8,64,256]{2,1,0:T(8,128)S(1)}, s32[]{:T(128)}) while((s32[]{:T(128)}, f32[72,264]{1,0:T(8,128)S(1)}, s32[8,2]{0,1:T(2,128)S(1)}, f32[8,64,256]{2,1,0:T(8,128)S(1)}, s32[]{:T(128)}) %tuple.282), condition=%wide.while_cond.1, body=%wide.while_body.1.sunk | while | flops 2 | bytes 131181 | solution.py:77
  174.5 16.0 %while.66 = (s32[]{:T(128)}, f32[80,272]{1,0:T(8,128)S(1)}, s32[8,2]{0,1:T(2,128)S(1)}, f32[8,72,264]{2,1,0:T(8,128)S(1)}, s32[]{:T(128)}) while((s32[]{:T(128)}, f32[80,272]{1,0:T(8,128)S(1)}, s32[8,2]{0,1:T(2,128)S(1)}, f32[8,72,264]{2,1,0:T(8,128)S(1)}, s32[]{:T(128)}) %tuple.266), condition=%wide.while_cond, body=%wide.while_body.sunk | while | flops 2 | bytes 221293 | solution.py:79
  191.2 15.9 %while.64 = (s32[]{:T(128)}, f32[72,264]{1,0:T(8,128)S(1)}, s32[8,2]{0,1:T(2,128)S(1)}, f32[8,64,256]{2,1,0:T(8,128)S(1)}, s32[]{:T(128)}) while((s32[]{:T(128)}, f32[72,264]{1,0:T(8,128)S(1)}, s32[8,2]{0,1:T(2,128)S(1)}, f32[8,64,256]{2,1,0:T(8,128)S(1)}, s32[]{:T(128)}) %tuple.260), condition=%wide.while_cond.2, body=%wide.while_body.2.sunk | while | flops 2 | bytes 131181 | solution.py:78
  207.1 15.9 %while.65 = (s32[]{:T(128)}, f32[72,264]{1,0:T(8,128)S(1)}, s32[8,2]{0,1:T(2,128)S(1)}, f32[8,64,256]{2,1,0:T(8,128)S(1)}, s32[]{:T(128)}) while((s32[]{:T(128)}, f32[72,264]{1,0:T(8,128)S(1)}, s32[8,2]{0,1:T(2,128)S(1)}, f32[8,64,256]{2,1,0:T(8,128)S(1)}, s32[]{:T(128)}) %tuple.282), condition=%wide.while_cond.1, body=%wide.while_body.1.sunk | while | flops 2 | bytes 131181 | solution.py:77
  224.6 16.0 %while.66 = (s32[]{:T(128)}, f32[80,272]{1,0:T(8,128)S(1)}, s32[8,2]{0,1:T(2,128)S(1)}, f32[8,72,264]{2,1,0:T(8,128)S(1)}, s32[]{:T(128)}) while((s32[]{:T(128)}, f32[80,272]{1,0:T(8,128)S(1)}, s32[8,2]{0,1:T(2,128)S(1)}, f32[8,72,264]{2,1,0:T(8,128)S(1)}, s32[]{:T(128)}) %tuple.266), condition=%wide.while_cond, body=%wide.while_body.sunk | while | flops 2 | bytes 221293 | solution.py:79
  241.3 15.9 %while.64 = (s32[]{:T(128)}, f32[72,264]{1,0:T(8,128)S(1)}, s32[8,2]{0,1:T(2,128)S(1)}, f32[8,64,256]{2,1,0:T(8,128)S(1)}, s32[]{:T(128)}) while((s32[]{:T(128)}, f32[72,264]{1,0:T(8,128)S(1)}, s32[8,2]{0,1:T(2,128)S(1)}, f32[8,64,256]{2,1,0:T(8,128)S(1)}, s32[]{:T(128)}) %tuple.260), condition=%wide.while_cond.2, body=%wide.while_body.2.sunk | while | flops 2 | bytes 131181 | solution.py:78
  257.2 15.9 %while.65 = (s32[]{:T(128)}, f32[72,264]{1,0:T(8,128)S(1)}, s32[8,2]{0,1:T(2,128)S(1)}, f32[8,64,256]{2,1,0:T(8,128)S(1)}, s32[]{:T(128)}) while((s32[]{:T(128)}, f32[72,264]{1,0:T(8,128)S(1)}, s32[8,2]{0,1:T(2,128)S(1)}, f32[8,64,256]{2,1,0:T(8,128)S(1)}, s32[]{:T(128)}) %tuple.282), condition=%wide.while_cond.1, body=%wide.while_body.1.sunk | while | flops 2 | bytes 131181 | solution.py:77
  274.7 16.0 %while.66 = (s32[]{:T(128)}, f32[80,272]{1,0:T(8,128)S(1)}, s32[8,2]{0,1:T(2,128)S(1)}, f32[8,72,264]{2,1,0:T(8,128)S(1)}, s32[]{:T(128)}) while((s32[]{:T(128)}, f32[80,272]{1,0:T(8,128)S(1)}, s32[8,2]{0,1:T(2,128)S(1)}, f32[8,72,264]{2,1,0:T(8,128)S(1)}, s32[]{:T(128)}) %tuple.266), condition=%wide.while_cond, body=%wide.while_body.sunk | while | flops 2 | bytes 221293 | solution.py:79
  291.3 15.9 %while.64 = (s32[]{:T(128)}, f32[72,264]{1,0:T(8,128)S(1)}, s32[8,2]{0,1:T(2,128)S(1)}, f32[8,64,256]{2,1,0:T(8,128)S(1)}, s32[]{:T(128)}) while((s32[]{:T(128)}, f32[72,264]{1,0:T(8,128)S(1)}, s32[8,2]{0,1:T(2,128)S(1)}, f32[8,64,256]{2,1,0:T(8,128)S(1)}, s32[]{:T(128)}) %tuple.260), condition=%wide.while_cond.2, body=%wide.while_body.2.sunk | while | flops 2 | bytes 131181 | solution.py:78
  307.3 15.9 %while.65 = (s32[]{:T(128)}, f32[72,264]{1,0:T(8,128)S(1)}, s32[8,2]{0,1:T(2,128)S(1)}, f32[8,64,256]{2,1,0:T(8,128)S(1)}, s32[]{:T(128)}) while((s32[]{:T(128)}, f32[72,264]{1,0:T(8,128)S(1)}, s32[8,2]{0,1:T(2,128)S(1)}, f32[8,64,256]{2,1,0:T(8,128)S(1)}, s32[]{:T(128)}) %tuple.282), condition=%wide.while_cond.1, body=%wide.while_body.1.sunk | while | flops 2 | bytes 131181 | solution.py:77
  324.7 16.0 %while.66 = (s32[]{:T(128)}, f32[80,272]{1,0:T(8,128)S(1)}, s32[8,2]{0,1:T(2,128)S(1)}, f32[8,72,264]{2,1,0:T(8,128)S(1)}, s32[]{:T(128)}) while((s32[]{:T(128)}, f32[80,272]{1,0:T(8,128)S(1)}, s32[8,2]{0,1:T(2,128)S(1)}, f32[8,72,264]{2,1,0:T(8,128)S(1)}, s32[]{:T(128)}) %tuple.266), condition=%wide.while_cond, body=%wide.while_body.sunk | while | flops 2 | bytes 221293 | solution.py:79
  341.4 15.9 %while.64 = (s32[]{:T(128)}, f32[72,264]{1,0:T(8,128)S(1)}, s32[8,2]{0,1:T(2,128)S(1)}, f32[8,64,256]{2,1,0:T(8,128)S(1)}, s32[]{:T(128)}) while((s32[]{:T(128)}, f32[72,264]{1,0:T(8,128)S(1)}, s32[8,2]{0,1:T(2,128)S(1)}, f32[8,64,256]{2,1,0:T(8,128)S(1)}, s32[]{:T(128)}) %tuple.260), condition=%wide.while_cond.2, body=%wide.while_body.2.sunk | while | flops 2 | bytes 131181 | solution.py:78
  357.3 15.9 %while.65 = (s32[]{:T(128)}, f32[72,264]{1,0:T(8,128)S(1)}, s32[8,2]{0,1:T(2,128)S(1)}, f32[8,64,256]{2,1,0:T(8,128)S(1)}, s32[]{:T(128)}) while((s32[]{:T(128)}, f32[72,264]{1,0:T(8,128)S(1)}, s32[8,2]{0,1:T(2,128)S(1)}, f32[8,64,256]{2,1,0:T(8,128)S(1)}, s32[]{:T(128)}) %tuple.282), condition=%wide.while_cond.1, body=%wide.while_body.1.sunk | while | flops 2 | bytes 131181 | solution.py:77
  374.8 16.0 %while.66 = (s32[]{:T(128)}, f32[80,272]{1,0:T(8,128)S(1)}, s32[8,2]{0,1:T(2,128)S(1)}, f32[8,72,264]{2,1,0:T(8,128)S(1)}, s32[]{:T(128)}) while((s32[]{:T(128)}, f32[80,272]{1,0:T(8,128)S(1)}, s32[8,2]{0,1:T(2,128)S(1)}, f32[8,72,264]{2,1,0:T(8,128)S(1)}, s32[]{:T(128)}) %tuple.266), condition=%wide.while_cond, body=%wide.while_body.sunk | while | flops 2 | bytes 221293 | solution.py:79
  475.2 383.3 %while.63 = (s32[]{:T(128)}, f32[64,256]{1,0:T(8,128)S(1)}, f32[64,256]{1,0:T(8,128)S(1)}, f32[64,256]{1,0:T(8,128)S(1)}, f32[64,256]{1,0:T(8,128)S(1)}, /*index...) while((s32[]{:T(128)}, f32[64,256]{1,0:T(8,128)S(1)}, ...), condition=%wide.region_15.16_spmd.clone, body=%wide.region_10.15_spmd.clone.sunk | while | flops 5460633 | bytes 17080092 | solution.py:166
  (1575 shorter events, 1267.7 us)
Async XLA Ops:
  2.3 20.2 %collective-permute-start = (f32[2,8,256]{2,1,0:T(8,128)S(1)}, f32[2,8,256]{2,1,0:T(8,128)S(1)}, u32[]{:S(2)}, u32[]{:S(2)}) collective-permute-start(f32[2,8,256]{2,1,0:T(8,128)S(1)} %get-tuple-element.748), channel_id=1, source_target_pairs={{0,1},{2,3},{4,5},{6,7},{8,9},{10,11},{12,13},{14,15},{16,17},{18,... | collective-permute-start | bytes 49160 | tf_op jit(solution)/shard_map/ppermute | solution.py:31
  4.7 17.8 %collective-permute-start.1 = (f32[2,8,256]{2,1,0:T(8,128)S(1)}, f32[2,8,256]{2,1,0:T(8,128)S(1)}, u32[]{:S(2)}, u32[]{:S(2)}) collective-permute-start(f32[2,8,256]{2,1,0:T(8,128)S(1)} %get-tuple-element.749), channel_id=1, source_target_pairs={{1,0},{3,2},{5,4},{7,6},{9,8},{11,10},{13,12},{15,14},{17,16},{19,... | collective-permute-start | bytes 49160 | tf_op jit(solution)/shard_map/ppermute | solution.py:33
  7.7 14.1 %copy-start.5 = (s32[8]{0:T(128)}, s32[8]{0:T(128)S(1)}, u32[]{:S(2)}) copy-start(s32[8]{0:T(128)S(1)} %get-tuple-element.597) | copy-start | bytes 100
  18.0 4.5 copy-start.7
  23.3 1.0 copy-start
  425.7 15.1 %all-to-all-start = ((f32[2,1,8,2048]{3,0,1,2:T(2,128)}), f32[2,1,8,2048]{3,0,1,2:T(2,128)S(1)}, u32[]{:S(2)}, u32[]{:S(2)}) async-start(f32[2,1,8,2048]{3,0,1,2:T(2,128)} %pad_maximum_fusion), calls=%async_computation | async-start | bytes 262144 | tf_op jit(solution)/shard_map/all_to_all | solution.py:171
  433.1 16.3 %copy-start.3 = (f32[128,128,1]{1,0,2:T(8,128)}, f32[128,128,1]{1,0,2:T(8,128)S(1)}, u32[]{:S(2)}) copy-start(f32[128,128,1]{1,0,2:T(8,128)S(1)} %convolution_bitcast_fusion.10) | copy-start | bytes 196612
  449.4 3.5 copy-start.6
  451.6 1.3 copy-start.1
  454.8 20.2 %all-to-all-start.1 = ((f32[2,8,1,2048]{3,0,2,1:T(2,128)}), f32[2,8,1,2048]{3,0,2,1:T(2,128)S(1)}, u32[]{:S(2)}, u32[]{:S(2)}) async-start(f32[2,8,1,2048]{3,0,2,1:T(2,128)} %copy.30), calls=%async_computation.1 | async-start | bytes 262144 | tf_op jit(solution)/shard_map/all_to_all | solution.py:183
  858.4 13.5 %copy-start.2 = (f32[2,128,2048]{1,2,0:T(8,128)S(1)}, f32[2,128,2048]{1,2,0:T(8,128)}, u32[]{:S(2)}) copy-start(f32[2,128,2048]{1,2,0:T(8,128)} %copy-done.1) | copy-start | bytes 6291460
  858.5 13.5 %copy-start.4 = (f32[128,128,1]{1,0,2:T(8,128)S(1)}, f32[128,128,1]{1,0,2:T(8,128)}, u32[]{:S(2)}) copy-start(f32[128,128,1]{1,0,2:T(8,128)} %copy-done.3) | copy-start | bytes 196612
  859.4 10.7 %all-to-all-start.2 = ((f32[2,1,8,2048]{3,0,1,2:T(2,128)}), f32[2,1,8,2048]{3,0,1,2:T(2,128)S(1)}, u32[]{:S(2)}, u32[]{:S(2)}) async-start(f32[2,1,8,2048]{3,0,1,2:T(2,128)} %pad_maximum_fusion.1), calls=%async_computation.2 | async-start | bytes 262144 | tf_op jit(solution)/shard_map/all_to_all | solution.py:171
where the time goes:
time: 898 us; the launch traced here: 884 us
  local copies, waits for them, and re-layouts  749 us (83%)
  other arithmetic  38.3 us (4%)
  matrix products  35.7 us (4%)
  starting transfers between devices  27.1 us (3%)
  waiting for transfers between devices  21.4 us (2%)
  loops' own time  10.8 us (1%)
    gather x1152, local copies, waits for them, and re-layouts  739 us
    reduce_max x16, other arithmetic, block_step(): new_max = jnp.maximum(running_max, jnp.max(match_scores, axis=0))  18.8 us
  transfers between devices with their start and end apart: 5, of which 3 were waited for; matrix products, arithmetic and copies ran while one was open for 2% of the time, Pallas kernels for 0%

commit v1 on v0

--- a/solution.py
+++ b/solution.py
@@ -1,6 +1,10 @@
+import functools
+
 import jax
 import jax.numpy as jnp
 from jax import lax
+from jax.experimental import pallas as pl
+from jax.experimental.pallas import tpu as pltpu
 from jax.sharding import PartitionSpec as P
 
 OFFSETS = 64
@@ -185,6 +189,477 @@
     return (sparse[:, :, None, :], motion[:, None])
 
 
+LANES = 128
+SUBLANES = 8
+GROUP = 4
+SPAN = 2 * SEARCH + 1
+WINDOW = 2 * RADIUS + 1
+SCALE = 1.4426950408889634 / SOFTMIN_HEAT
+
+
+def pack_kernel(first, second, prior, edge, out, ext_first, ext_second, *, rows_axis, strip, blocks):
+    margin = SEARCH + RADIUS
+    band = first.shape[0]
+    here = lax.axis_index(rows_axis)
+    count = lax.axis_size(rows_axis)
+    none = jnp.zeros((margin, first.shape[1]), jnp.float32)
+    for slot, (source, ext) in enumerate(((first, ext_first), (second, ext_second))):
+        got = edge[slot]
+        ext[0:margin, :] = jnp.where(here > 0, got, none)
+        ext[margin : margin + band, :] = source[...]
+        ext[margin + band : band + 2 * margin, :] = jnp.where(here < count - 1, got, none)
+    tiles = first.shape[1] // LANES
+    per = 5 * strip + 2 * RADIUS + 2 * margin - strip
+    tall = strip + 2 * RADIUS
+    taller = strip + 2 * margin
+    for block in range(blocks):
+        for tile in range(tiles):
+            lanes = slice(tile * LANES, (tile + 1) * LANES)
+            at = (block * tiles + tile) * per
+            top = block * strip
+            out[at : at + tall, :] = ext_first[top + SEARCH : top + SEARCH + tall, lanes]
+            at += tall
+            out[at : at + taller, :] = ext_second[top : top + taller, lanes]
+            at += taller
+            out[at : at + strip, :] = prior[0, top : top + strip, lanes]
+            at += strip
+            out[at : at + strip, :] = prior[1, top : top + strip, lanes]
+
+
+def window_sums(rows):
+    count = len(rows)
+    twos = [rows[a] + rows[a + 1] for a in range(count - 1)]
+    fours = [twos[a] + twos[a + 2] for a in range(count - 3)]
+    eights = [fours[a] + fours[a + 4] for a in range(count - 7)]
+    return [eights[a] + rows[a + 8] for a in range(count - 8)]
+
+
+def store_split(parts, at, lanes, upper, lower):
+    value = jnp.concatenate((upper, lower), axis=0)
+    high = value.astype(jnp.bfloat16)
+    rest = value - high.astype(jnp.float32)
+    mid = rest.astype(jnp.bfloat16)
+    low = (rest - mid.astype(jnp.float32)).astype(jnp.bfloat16)
+    for part, piece in enumerate((high, mid, low)):
+        parts[part, at : at + 2 * SUBLANES, lanes] = piece
+
+
+def split_dot(parts, right):
+    total = jnp.dot(parts[0], right, preferred_element_type=jnp.float32)
+    total = total + jnp.dot(parts[1], right, preferred_element_type=jnp.float32)
+    return total + jnp.dot(parts[2], right, preferred_element_type=jnp.float32)
+
+
+def lane_shift(tiles, edge, shift, lane):
+    if shift == 0:
+        return tiles
+    rolled = [pltpu.roll(tile, (-shift) % LANES, 1) for tile in tiles]
+    outer = jnp.zeros_like(tiles[0]) if edge is None else pltpu.roll(edge, (-shift) % LANES, 1)
+    if shift > 0:
+        keep = lane < LANES - shift
+        following = rolled[1:] + [outer]
+        return [jnp.where(keep, own, other) for own, other in zip(rolled, following)]
+    keep = lane >= -shift
+    before = [outer] + rolled[:-1]
+    return [jnp.where(keep, own, other) for own, other in zip(rolled, before)]
+
+
+def track_kernel(
+    offsets,
+    pair_epochs,
+    pair_slot,
+    data,
+    velocity,
+    motion,
+    band,
+    stat_parts,
+    parts,
+    first,
+    second,
+    mean_first,
+    scale_first,
+    mean_second,
+    scale_second,
+    table,
+    prior,
+    matched,
+    predicted,
+    sparse,
+    spread,
+    running,
+    steps,
+    inverse,
+    lengths,
+    order,
+    bounds,
+):
+    strip = SUBLANES
+    margin = SEARCH + RADIUS
+    tall = strip + 2 * RADIUS
+    taller = strip + 2 * margin
+    per = tall + taller + 2 * strip
+    wide = strip + 2 * SEARCH
+    area = float(WINDOW * WINDOW)
+    count = pair_slot.shape[0]
+    columns = band.shape[0]
+    tiles = columns // LANES
+    cells = strip * tiles
+    lane = lax.broadcasted_iota(jnp.int32, (SUBLANES, LANES), 1)
+
+    tap = lax.broadcasted_iota(jnp.int32, band.shape, 0)
+    column = lax.broadcasted_iota(jnp.int32, band.shape, 1)
+    centre = jnp.where(column < columns + LANES // 2, column, column - columns - LANES)
+    band[...] = jnp.where(jnp.abs(tap - centre) <= RADIUS, 1.0, 0.0).astype(jnp.bfloat16)
+
+    def fetch(row, tile):
+        return data[pl.ds(tile * per + row, SUBLANES, stride=tiles * per), :]
+
+    for component in range(2):
+        for row in range(strip):
+            for tile in range(tiles):
+                prior[component * cells + row * tiles + tile] = fetch(tall + taller + component * strip + row, tile)
+
+    for tile in range(tiles):
+        lanes = slice(tile * LANES, (tile + 1) * LANES)
+        rows = [fetch(row, tile) for row in range(tall)]
+        for row in range(tall):
+            first[row * tiles + tile] = rows[row]
+        at = 0
+        for values in (rows, [row * row for row in rows]):
+            sums = window_sums(values)
+            for row in range(0, strip, 2):
+                store_split(stat_parts, at, lanes, sums[row], sums[row + 1])
+                at += 2 * SUBLANES
+        rows = [fetch(tall + row, tile) for row in range(taller)]
+        for values in (rows, [row * row for row in rows]):
+            sums = window_sums(values)
+            for row in range(0, wide, 2):
+                store_split(stat_parts, at, lanes, sums[row], sums[row + 1])
+                at += 2 * SUBLANES
+    for row in range(taller):
+        pieces = [fetch(tall + row, tile) for tile in range(tiles)]
+        for shift in range(-SEARCH, SEARCH + 1):
+            moved = lane_shift(pieces, None, shift, lane)
+            for tile in range(tiles):
+                second[((shift + SEARCH) * taller + row) * tiles + tile] = moved[tile]
+    sums = split_dot(stat_parts, band[...])
+    for row in range(strip):
+        for tile in range(tiles):
+            lanes = slice(tile * LANES, (tile + 1) * LANES)
+            total = sums[row * SUBLANES : (row + 1) * SUBLANES, lanes]
+            squares = sums[(strip + row) * SUBLANES : (strip + row + 1) * SUBLANES, lanes] / area
+            mean = total / area
+            mean_first[row * tiles + tile] = total
+            scale_first[row * tiles + tile] = lax.rsqrt(
+                jnp.maximum(squares - mean * mean, VARIANCE_FLOOR)
+            ) * (SCALE / area)
+    for row in range(wide):
+        means, scales = [], []
+        for tile in range(tiles + 1):
+            lanes = slice(tile * LANES, (tile + 1) * LANES)
+            at = (2 * strip + row) * SUBLANES
+            mean = sums[at : at + SUBLANES, lanes] / area
+            at = (2 * strip + wide + row) * SUBLANES
+            squares = sums[at : at + SUBLANES, lanes] / area
+            means.append(mean)
+            scales.append(lax.rsqrt(jnp.maximum(squares - mean * mean, VARIANCE_FLOOR)))
+        for shift in range(-SEARCH, SEARCH + 1):
+            for values, held in ((means, mean_second), (scales, scale_second)):
+                moved = lane_shift(values[:tiles], values[tiles], shift, lane)
+                for tile in range(tiles):
+                    held[((shift + SEARCH) * wide + row) * tiles + tile] = moved[tile]
+
+    nothing = jnp.zeros((SUBLANES, LANES), jnp.float32)
+
+    def clear(index, carry):
+        table[index] = nothing
+        return carry
+
+    lax.fori_loop(0, SPAN * SPAN * cells, clear, 0, unroll=8)
+
+    def offset_group(group, carry):
+        places = []
+        for member in range(GROUP):
+            row_shift = offsets[group * GROUP + member, 0] + SEARCH
+            column_shift = offsets[group * GROUP + member, 1] + SEARCH
+            places.append((row_shift, column_shift))
+            at_second = (column_shift * taller + row_shift) * tiles
+            for tile in range(tiles):
+                lanes = slice(tile * LANES, (tile + 1) * LANES)
+                products = [
+                    first[row * tiles + tile] * second[at_second + row * tiles + tile]
+                    for row in range(tall)
+                ]
+                sums = window_sums(products)
+                for row in range(0, strip, 2):
+                    at = member * strip * SUBLANES + row * SUBLANES
+                    store_split(parts, at, lanes, sums[row], sums[row + 1])
+        crossed = split_dot(parts, band[:, 0:columns])
+        for member in range(GROUP):
+            row_shift, column_shift = places[member]
+            at_second = (column_shift * wide + row_shift) * tiles
+            at_table = (column_shift * SPAN + row_shift) * cells
+            for row in range(strip):
+                for tile in range(tiles):
+                    at = (member * strip + row) * SUBLANES
+                    cell = row * tiles + tile
+                    total = crossed[at : at + SUBLANES, tile * LANES : (tile + 1) * LANES]
+                    covariance = total - mean_first[cell] * mean_second[at_second + cell]
+                    scaled = covariance * (scale_first[cell] * scale_second[at_second + cell])
+                    table[at_table + cell] = jnp.exp2(scaled)
+        return carry
+
+    lax.fori_loop(0, offsets.shape[0] // GROUP, offset_group, 0)
+
+    ends = [pair_epochs[pair_slot[j], 0] for j in range(count)]
+    ends += [pair_epochs[pair_slot[j], 1] for j in range(count)]
+    ranks = [jnp.int32(0)] * (2 * count)
+    for a in range(2 * count):
+        for b in range(a + 1, 2 * count):
+            ahead = (ends[a] <= ends[b]).astype(jnp.int32)
+            ranks[b] = ranks[b] + ahead
+            ranks[a] = ranks[a] + (1 - ahead)
+    for a in range(2 * count):
+        order[ranks[a]] = a
+        bounds[ranks[a]] = ends[a]
+    segments = 2 * count - 1
+    for s in range(segments):
+        lengths[s] = jnp.full((SUBLANES, LANES), (bounds[s + 1] - bounds[s]).astype(jnp.float32))
+
+    gram = [[None] * count for _ in range(count)]
+    for a in range(count):
+        for b in range(a, count):
+            shared = jnp.minimum(ends[count + a], ends[count + b]) - jnp.maximum(ends[a], ends[b])
+            value = jnp.maximum(shared, 0).astype(jnp.float32) + (PENALTY if a == b else 0.0)
+            gram[a][b] = gram[b][a] = jnp.full((SUBLANES, LANES), value)
+    for k in range(count):
+        pivot = 1.0 / gram[k][k]
+        scaled = [gram[k][b] * pivot for b in range(count)]
+        for a in range(count):
+            if a == k:
+                continue
+            factor = gram[a][k]
+            for b in range(count):
+                if b != k:
+                    gram[a][b] = gram[a][b] - factor * scaled[b]
+            gram[a][k] = -(factor * pivot)
+        for b in range(count):
+            gram[k][b] = scaled[b]
+        gram[k][k] = pivot
+    for a in range(count):
+        for b in range(count):
+            inverse[a * count + b] = gram[a][b]
+
+    halves = cells // SUBLANES
+    groups = 2 * halves
+    threshold = SPARSITY / PENALTY
+
+    def match(first_guess):
+        def pixel_tile(cell, carry):
+            guess = []
+            for component in range(2):
+                value = prior[component * cells + cell]
+                if not first_guess:
+                    at = pl.multiple_of((component * cells + cell) * SUBLANES, SUBLANES)
+                    value = 0.5 * (value + predicted[pl.ds(at, SUBLANES), :])
+                guess.append(value)
+            factors = []
+            for value in guess:
+                nearest = jnp.clip(jnp.round(value), -float(SEARCH), float(SEARCH))
+                peak = nearest * value - 0.5 * nearest * nearest
+                factors.append(
+                    [
+                        jnp.exp(value * float(shift) - (peak + 0.5 * shift * shift))
+                        for shift in range(-SEARCH, SEARCH + 1)
+                    ]
+                )
+            weight = row_moment = column_moment = None
+            for column_shift in range(SPAN):
+                part = moment = None
+                for row_shift in range(SPAN):
+                    term = factors[0][row_shift] * table[(column_shift * SPAN + row_shift) * cells + cell]
+                    lever = term * float(row_shift - SEARCH)
+                    part = term if part is None else part + term
+                    if row_shift != SEARCH:
+                        moment = lever if moment is None else moment + lever
+                factor = factors[1][column_shift]
+                part = part * factor
+                moment = moment * factor
+                lever = part * float(column_shift - SEARCH)
+                weight = part if weight is None else weight + part
+                row_moment = moment if row_moment is None else row_moment + moment
+                column_moment = lever if column_moment is None else column_moment + lever
+            share = 1.0 / weight
+            for component, value in enumerate((row_moment, column_moment)):
+                at = pl.multiple_of((component * cells + cell) * SUBLANES, SUBLANES)
+                matched[pl.ds(at, SUBLANES), :] = value * share
+            return carry
+
+        lax.fori_loop(0, cells, pixel_tile, 0)
+
+    def across(group, j):
+        return pl.ds(group * SUBLANES * SUBLANES + j, SUBLANES, stride=SUBLANES)
+
+    starts = ranks[:count]
+    finishes = ranks[count:]
+
+    def invert():
+        def iterate(iteration, carry):
+            for group in range(groups):
+                total = nothing
+                running[group, 0] = total
+                for s in range(segments):
+                    total = total + lengths[s] * spread[group, s]
+                    running[group, s + 1] = total
+                residual = [
+                    matched[across(group, j), :]
+                    - (running[group, finishes[j]] - running[group, starts[j]])
+                    for j in range(count)
+                ]
+                for a in range(count):
+                    step = inverse[a * count] * residual[0]
+                    for b in range(1, count):
+                        step = step + inverse[a * count + b] * residual[b]
+                    steps[group, a] = step
+                    steps[group, count + a] = -step
+                level = nothing
+                for s in range(segments):
+                    level = level + steps[group, order[s]]
+                    blended = sparse[group, s + 1] + level
+                    scaled = jnp.clip(blended, -threshold, threshold)
+                    shrunk = blended - scaled
+                    sparse[group, s + 1] = shrunk
+                    spread[group, s] = shrunk - scaled
+            return carry
+
+        lax.fori_loop(0, ITERS, iterate, 0)
+
+    for group in range(groups):
+        for s in range(segments):
+            spread[group, s] = nothing
+        for s in range(segments + 2):
+            sparse[group, s] = nothing
+    for round_number in range(ROUNDS):
+        match(round_number == 0)
+        invert()
+        if round_number + 1 < ROUNDS:
+            for group in range(groups):
+                total = nothing
+                running[group, 0] = total
+                for s in range(segments):
+                    total = total + lengths[s] * sparse[group, s + 1]
+                    running[group, s + 1] = total
+                for j in range(count):
+                    predicted[across(group, j), :] = (
+                        running[group, finishes[j]] - running[group, starts[j]]
+                    )
+
+    for j in range(count):
+        for component in range(2):
+            for tile in range(tiles):
+                at = (component * cells + tile) * SUBLANES + j
+                motion[j, component, :, tile * LANES : (tile + 1) * LANES] = matched[
+                    pl.ds(at, SUBLANES, stride=tiles * SUBLANES), :
+                ]
+
+    def fill(low, high, s):
+        held = [sparse[group, s] for group in range(groups)]
+
+        def one(epoch, carry):
+            for group in range(groups):
+                half = group % halves
+                velocity[group // halves, epoch, half * SUBLANES : (half + 1) * SUBLANES, :] = held[group]
+            return carry
+
+        lax.fori_loop(low, high, one, 0)
+
+    epochs = velocity.shape[1]
+    fill(0, bounds[0], 0)
+    for s in range(segments):
+        fill(bounds[s], bounds[s + 1], s + 1)
+    fill(bounds[segments], epochs, segments + 1)
+
+
+def by_strips(first_image, second_image, prior_motion, offsets, pair_epochs, pair_slot):
+    band_rows, columns = first_image.shape[1:]
+    margin = SEARCH + RADIUS
+    count = lax.axis_size("pairs")
+    strip = band_rows // count
+    tiles = columns // LANES
+    cells = strip * tiles
+    tall = strip + 2 * RADIUS
+    taller = strip + 2 * margin
+    wide = strip + 2 * SEARCH
+    per = tall + taller + 2 * strip
+    here = lax.axis_index("rows")
+    start = jnp.where(here == 0, band_rows - margin, 0)
+    images = (first_image[0], second_image[0])
+    edge = jnp.stack([lax.dynamic_slice(image, (start, 0), (margin, columns)) for image in images])
+    edge = lax.ppermute(edge, "rows", [(0, 1), (1, 0)])
+    packed = pl.pallas_call(
+        functools.partial(pack_kernel, rows_axis="rows", strip=strip, blocks=count),
+        out_shape=jax.ShapeDtypeStruct((count * tiles * per, LANES), jnp.float32),
+        scratch_shapes=[pltpu.VMEM((band_rows + 2 * margin, columns), jnp.float32)] * 2,
+    )(first_image[0], second_image[0], prior_motion[:, 0], edge)
+    arrived = lax.all_to_all(packed, "pairs", split_axis=0, concat_axis=0, tiled=True)
+    tile = lambda *lead: pltpu.VMEM((*lead, SUBLANES, LANES), jnp.float32)
+    flat = lambda rows: pltpu.VMEM((rows * SUBLANES, LANES), jnp.float32)
+    groups = 2 * cells // SUBLANES
+    stat_rows = (2 * strip + 2 * wide) * SUBLANES
+    smem = pl.BlockSpec(memory_space=pltpu.SMEM)
+    vmem = pl.BlockSpec(memory_space=pltpu.VMEM)
+    velocity, motion = pl.pallas_call(
+        track_kernel,
+        out_shape=(
+            jax.ShapeDtypeStruct((2, EPOCHS, cells, LANES), jnp.float32),
+            jax.ShapeDtypeStruct((count, 2, strip, columns), jnp.float32),
+        ),
+        in_specs=[smem, smem, smem, vmem],
+        out_specs=(vmem, vmem),
+        scratch_shapes=[
+            pltpu.VMEM((columns, columns + LANES), jnp.bfloat16),
+            pltpu.VMEM((3, stat_rows, columns), jnp.bfloat16),
+            pltpu.VMEM((3, GROUP * strip * SUBLANES, columns), jnp.bfloat16),
+            tile(tall * tiles),
+            tile(SPAN * taller * tiles),
+            tile(cells),
+            tile(cells),
+            tile(SPAN * wide * tiles),
+            tile(SPAN * wide * tiles),
+            tile(SPAN * SPAN * cells),
+            tile(2 * cells),
+            flat(2 * cells),
+            flat(2 * cells),
+            tile(groups, 2 * count + 1),
+            tile(groups, 2 * count - 1),
+            tile(groups, 2 * count),
+            tile(groups, 2 * count),
+            tile(count * count),
+            tile(2 * count - 1),
+            pltpu.SMEM((2 * count,), jnp.int32),
+            pltpu.SMEM((2 * count,), jnp.int32),
+        ],
+        compiler_params=pltpu.CompilerParams(vmem_limit_bytes=48 * 1024 * 1024),
+    )(offsets, pair_epochs, pair_slot, arrived)
+    returned = lax.all_to_all(motion, "pairs", split_axis=0, concat_axis=0, tiled=True)
+    returned = jnp.moveaxis(returned, 0, 1).reshape(2, 1, band_rows, columns)
+    return (velocity.reshape(2, EPOCHS, 1, strip * columns), returned)
+
+
+def per_device_any(first_image, second_image, *rest):
+    band_rows, columns = first_image.shape[1:]
+    count = lax.axis_size("pairs")
+    strips = (
+        count == SUBLANES
+        and band_rows == count * SUBLANES
+        and columns == 2 * LANES
+        and lax.axis_size("rows") == 2
+        and rest[1].shape[0] % GROUP == 0
+    )
+    plan = by_strips if strips else per_device
+    return plan(first_image, second_image, *rest)
+
+
 def solution(mesh):
     placed = (
         P(("groups", "pairs"), "rows", None),
@@ -195,7 +670,7 @@
         P("groups"),
     )
     return jax.shard_map(
-        per_device,
+        per_device_any,
         mesh=mesh,
         in_specs=placed,
         out_specs=(

time: 898 us -> 54 us (0.06); the launches traced: 884 us -> 53.6 us
  local copies, waits for them, and re-layouts: 749 us -> 4.16 us
  other arithmetic: 38.3 us -> 0.01 us
  matrix products: 35.7 us -> 0 us
  starting transfers between devices: 27.1 us -> 7.63 us
  Pallas kernels: 0 us -> 17.7 us
  loops' own time: 10.8 us -> 0 us
  blocking collectives: 0 us -> 10.8 us
    gather x1152 -> x0, local copies, waits for them, and re-layouts: 739 us -> none
    dot_general x76 -> x0, matrix products: 35.7 us -> none  [the longest x8 16.9 us: per_device(): jnp.einsum('ef,cfn->cen', inverse_matrix, target, precision=HIGHEST)]
    reduce_max x17 -> x0, other arithmetic: 19.4 us -> none  [the longest x16 18.8 us: block_step(): new_max = jnp.maximum(running_max, jnp.max(match_scores, axis=0))]
    pallas_call x0 -> x2, Pallas kernels: none -> 17.7 us  [the longest x1 15.9 us: by_strips(): pl.pallas_call(track_kernel, out_shape=(jax.ShapeDtypeStruct((2, EPOCHS,...]
    all_to_all x3 -> x1, starting transfers between devices: 23.4 us -> 7.13 us  [by_strips(): lax.all_to_all(packed, 'pairs', split_axis=0, concat_axis=0, tiled=True)]
    all_to_all x0 -> x1, blocking collectives: none -> 10.8 us  [by_strips(): lax.all_to_all(motion, 'pairs', split_axis=0, concat_axis=0, tiled=True)]
    another operation x50 -> x0, loops' own time: 10.8 us -> none  [the longest x16 3.01 us: correlate(): lax.dynamic_slice(second_padded, (row_start, col_start), (height + 2 * RA...]
    add x35 -> x0, other arithmetic: 10.5 us -> none  [the longest x19 9.5 us: box_sum(): running = running + values[..., position:position + height, :]]
  transfers between devices with their start and end apart: 5 -> 2, of which waited for: 3 -> 2; matrix products, arithmetic and copies ran while one was open for 2% -> 3% of each run, Pallas kernels for 0% -> 0%
where the time goes in v1:
time: 54 us; the launch traced here: 53.6 us
  Pallas kernels  17.7 us (33%)
  waiting for transfers between devices  12.7 us (24%)
  blocking collectives  10.8 us (20%)
  starting transfers between devices  7.63 us (14%)
  local copies, waits for them, and re-layouts  4.16 us (8%)
  between operations  0.64 us (1%)
    pallas_call x1, Pallas kernels, by_strips(): pl.pallas_call(track_kernel, out_shape=(jax.ShapeDtypeStruct((2, EPOCHS,...  15.9 us
    all_to_all x1, waiting for transfers between devices, by_strips(): lax.all_to_all(packed, 'pairs', split_axis=0, concat_axis=0, tiled=True)  11.9 us
    all_to_all x1, blocking collectives, by_strips(): lax.all_to_all(motion, 'pairs', split_axis=0, concat_axis=0, tiled=True)  10.8 us
    all_to_all x1, starting transfers between devices, by_strips(): lax.all_to_all(packed, 'pairs', split_axis=0, concat_axis=0, tiled=True)  7.13 us
    unnamed x7, local copies, waits for them, and re-layouts  3.44 us
    pallas_call x1, Pallas kernels, by_strips(): pl.pallas_call(functools.partial(pack_kernel, rows_axis='rows', strip=str...  1.79 us
  transfers between devices with their start and end apart: 2, of which 2 were waited for; matrix products, arithmetic and copies ran while one was open for 3% of the time, Pallas kernels for 0%

profile of v1, /device:TPU:0, one launch (start us, length us, event | category | flops | bytes accessed | tf_op | source)
XLA Modules:
  0.0 53.6 jit_solution(2694570914806015187)
XLA Ops:
  0.6 0.7 %constant_dynamic-slice_fusion = (f32[1,8,256]{2,1,0:T(8,128)S(1)}, f32[1,8,256]{2,1,0:T(8,128)S(1)}) fusion(f32[1,64,256]{2,1,0:T(8,128)} %param.7, s32[]{:T(128)S(6)} %select_n.6, f32[1,64,256]{2,1,0:T(8,128)} %param.6), kind=kLoop, calls=%fused_computation.2 | loop fusion | bytes 32772 | tf_op jit(solution)/shard_map/dynamic_slice | solution.py:597
  1.4 0.5 collective-permute-start
  1.9 0.8 %collective-permute-done.edge = f32[2,8,256]{2,1,0:T(8,128)S(1)} collective-permute-done((f32[2,8,256]{2,1,0:T(8,128)S(1)}, f32[2,8,256]{2,1,0:T(8,128)S(1)}, u32[]{:S(2)}, u32[]{:S(2)}) %collective-permute-start) | collective-permute-done | bytes 16416 | tf_op jit(solution)/shard_map/ppermute | solution.py:598
  2.7 0.0 copy-start.1
  2.7 0.6 %copy-done.1 = f32[2,8,256]{2,1,0:T(8,128)} copy-done((f32[2,8,256]{2,1,0:T(8,128)}, f32[2,8,256]{2,1,0:T(8,128)S(1)}, u32[]{:S(2)}) %copy-start.1) | copy-done | bytes 16408
  3.3 1.8 %shard_map.77 = f32[896,128]{1,0:T(8,128)} custom-call(f32[64,256]{1,0:T(8,128)} %bitcast.16, f32[64,256]{1,0:T(8,128)} %bitcast.17, f32[2,64,256]{2,1,0:T(8,128)} %bitcast.15, f32[2,8,256]{2,1,0:T(8,128)} %copy-done.1), custom_call_target="tpu_custom_call" | custom-call | tf_op jit(solution)/shard_map/pallas_call | solution.py:599
  5.1 7.1 %all-to-all-start = ((f32[8,112,128]{2,1,0:T(8,128)}), f32[8,112,128]{2,1,0:T(8,128)S(1)}, u32[]{:S(2)}, u32[]{:S(2)}) async-start(f32[8,112,128]{2,1,0:T(8,128)} %bitcast.14), calls=%async_computation | async-start | bytes 917504 | tf_op jit(solution)/shard_map/all_to_all | solution.py:604
  12.2 0.8 %copy.12.pair_epochs = s32[8,2]{1,0:T(8,128)S(1)} copy(s32[8,2]{0,1:T(2,128)} %param.10) | data formatting | bytes 128 | tf_op args[4]
  13.0 0.8 %copy.11.offsets = s32[64,2]{1,0:T(8,128)S(1)} copy(s32[64,2]{0,1:T(2,128)} %param.9) | data formatting | bytes 1024 | tf_op args[3]
  13.7 11.9 %all-to-all-done = f32[8,112,128]{2,1,0:T(8,128)S(1)} async-done(((f32[8,112,128]{2,1,0:T(8,128)}), f32[8,112,128]{2,1,0:T(8,128)S(1)}, u32[]{:S(2)}, u32[]{:S(2)}) %all-to-all-start) | async-done | bytes 458784 | tf_op jit(solution)/shard_map/all_to_all | solution.py:604
  25.6 0.0 copy-start
  25.6 0.7 %copy-done = s32[8]{0:T(128)S(1)} copy-done((s32[8]{0:T(128)S(1)}, s32[8]{0:T(128)}, u32[]{:S(2)}) %copy-start) | copy-done | bytes 56
  26.3 15.9 %shard_map.78 = (f32[2,128,16,128]{3,2,1,0:T(8,128)}, f32[8,2,8,256]{3,2,1,0:T(8,128)S(1)}) custom-call(s32[64,2]{1,0:T(8,128)S(1)} %copy.11.offsets, s32[8,2]{1,0:T(8,128)S(1)} %copy.12.pair_epochs, s32[8]{0:T(128)S(1)} %copy-done, f32[896,128]{1,0:T(8,128)S(1)} %bitcast.13), custom_call_target="tpu_custom_call" | custom-call | tf_op jit(solution)/shard_map/pallas_call | solution.py:611
  42.2 10.8 %all_to_all.16 = f32[8,2,8,256]{3,2,1,0:T(8,128)S(1)} all-to-all(f32[8,2,8,256]{3,2,1,0:T(8,128)S(1)} %get-tuple-element.5), channel_id=1, replica_groups=mesh['groups'=2,'pairs'=8,'rows'=2] {'pairs'}, dimensions={0} | all-to-all | bytes 262144 | tf_op jit(solution)/shard_map/all_to_all | solution.py:644
  52.9 0.7 %copy_bitcast_fusion = f32[2,1,64,256]{3,2,1,0:T(8,128)} fusion(f32[8,2,8,256]{3,2,1,0:T(8,128)S(1)} %all_to_all.16), kind=kLoop, calls=%fused_computation | loop fusion | bytes 262144
  (1 shorter events, 0.0 us)
Async XLA Ops:
  1.4 1.3 %collective-permute-start = (f32[2,8,256]{2,1,0:T(8,128)S(1)}, f32[2,8,256]{2,1,0:T(8,128)S(1)}, u32[]{:S(2)}, u32[]{:S(2)}) collective-permute-start(f32[2,8,256]{2,1,0:T(8,128)S(1)} %pad_maximum_fusion), channel_id=1, source_target_pairs={{0,1},{1,0},{2,3},{3,2},{4,5},{5,4},{6,7},{7,6},{8,9},{9,8},{10,11... | collective-permute-start | bytes 49160 | tf_op jit(solution)/shard_map/ppermute | solution.py:598
  2.7 0.6 %copy-start.1 = (f32[2,8,256]{2,1,0:T(8,128)}, f32[2,8,256]{2,1,0:T(8,128)S(1)}, u32[]{:S(2)}) copy-start(f32[2,8,256]{2,1,0:T(8,128)S(1)} %collective-permute-done.edge) | copy-start | bytes 49156
  5.1 20.5 %all-to-all-start = ((f32[8,112,128]{2,1,0:T(8,128)}), f32[8,112,128]{2,1,0:T(8,128)S(1)}, u32[]{:S(2)}, u32[]{:S(2)}) async-start(f32[8,112,128]{2,1,0:T(8,128)} %bitcast.14), calls=%async_computation | async-start | bytes 917504 | tf_op jit(solution)/shard_map/all_to_all | solution.py:604
  25.6 0.7 %copy-start = (s32[8]{0:T(128)S(1)}, s32[8]{0:T(128)}, u32[]{:S(2)}) copy-start(s32[8]{0:T(128)} %pair_slot.1) | copy-start | bytes 100

commit v2 on v0

--- a/solution.py
+++ b/solution.py
@@ -1,6 +1,10 @@
+import functools
+
 import jax
 import jax.numpy as jnp
 from jax import lax
+from jax.experimental import pallas as pl
+from jax.experimental.pallas import tpu as pltpu
 from jax.sharding import PartitionSpec as P
 
 OFFSETS = 64
@@ -185,6 +189,646 @@
     return (sparse[:, :, None, :], motion[:, None])
 
 
+LANES = 128
+SUBLANES = 8
+GROUP = 4
+SPAN = 2 * SEARCH + 1
+WINDOW = 2 * RADIUS + 1
+SCALE = 1.4426950408889634 / SOFTMIN_HEAT
+
+
+def strip_rows(strip):
+    tall = strip + 2 * RADIUS
+    taller = strip + 2 * (SEARCH + RADIUS)
+    return tall, taller, tall + taller + 2 * strip
+
+
+def pack_kernel(first_in, second_in, prior_in, out, first, second, prior, arrivals):
+    copies = [
+        pltpu.make_async_copy(source, target, arrivals.at[k])
+        for k, (source, target) in enumerate(((first_in, first), (second_in, second), (prior_in, prior)))
+    ]
+    for copy in copies:
+        copy.start()
+    band, columns = first.shape
+    strip = SUBLANES
+    tall, taller, per = strip_rows(strip)
+    tiles = columns // LANES
+
+    def windows(source, offset, reach, height):
+        for block in range(band // strip):
+            for tile in range(tiles):
+                lanes = slice(tile * LANES, (tile + 1) * LANES)
+                at = (block * tiles + tile) * per + offset
+                low = block * strip - reach
+                start, stop = max(low, 0), min(low + height, band)
+                if start > low:
+                    out[at : at + start - low, :] = jnp.zeros((start - low, LANES), jnp.float32)
+                out[at + start - low : at + stop - low, :] = source[start:stop, lanes]
+                if stop < low + height:
+                    out[at + stop - low : at + height, :] = jnp.zeros((low + height - stop, LANES), jnp.float32)
+
+    copies[0].wait()
+    windows(first, 0, RADIUS, tall)
+    copies[1].wait()
+    windows(second, tall, SEARCH + RADIUS, taller)
+    copies[2].wait()
+    for component in range(2):
+        windows(prior.at[component], tall + taller + component * strip, 0, strip)
+
+
+def patch_kernel(other_first, other_second, packed, out, edge, departures):
+    band, columns = other_first.shape
+    strip = SUBLANES
+    tall, taller, per = strip_rows(strip)
+    tiles = columns // LANES
+    blocks = band // strip
+    here = lax.axis_index("rows")
+    size = tiles * per
+    last = blocks - 1
+    rows_of = lambda block: pl.ds(pl.multiple_of(block * size, strip), size)
+    copies = [
+        pltpu.make_async_copy(
+            packed.at[pl.ds(size, (blocks - 2) * size)], out.at[pl.ds(size, (blocks - 2) * size)], departures.at[0]
+        ),
+        pltpu.make_async_copy(packed.at[rows_of(here * last)], out.at[rows_of(here * last)], departures.at[1]),
+    ]
+    for copy in copies:
+        copy.start()
+    edge[...] = packed[rows_of((1 - here) * last), :]
+    for tile in range(tiles):
+        lanes = slice(tile * LANES, (tile + 1) * LANES)
+        at = tile * per
+
+        @pl.when(here > 0)
+        def _():
+            edge[at : at + RADIUS, :] = other_first[band - RADIUS :, lanes]
+            edge[at + tall : at + tall + strip, :] = other_second[band - strip :, lanes]
+
+        @pl.when(here == 0)
+        def _():
+            edge[at + tall - RADIUS : at + tall, :] = other_first[:RADIUS, lanes]
+            edge[at + tall + taller - strip : at + tall + taller, :] = other_second[:strip, lanes]
+
+    copies.append(pltpu.make_async_copy(edge, out.at[rows_of((1 - here) * last)], departures.at[2]))
+    copies[2].start()
+    for copy in copies:
+        copy.wait()
+
+
+def window_sums(rows):
+    count = len(rows)
+    twos = [rows[a] + rows[a + 1] for a in range(count - 1)]
+    fours = [twos[a] + twos[a + 2] for a in range(count - 3)]
+    eights = [fours[a] + fours[a + 4] for a in range(count - 7)]
+    return [eights[a] + rows[a + 8] for a in range(count - 8)]
+
+
+def split_rows(upper, lower):
+    value = jnp.concatenate((upper, lower), axis=0)
+    high = value.astype(jnp.bfloat16)
+    rest = value - high.astype(jnp.float32)
+    mid = rest.astype(jnp.bfloat16)
+    low = (rest - mid.astype(jnp.float32)).astype(jnp.bfloat16)
+    return high, mid, low
+
+
+def lane_shift(tiles, edge, shift, lane):
+    if shift > 0:
+        tiles = [jnp.where(lane < shift, after, own) for own, after in zip(tiles, tiles[1:] + [edge])]
+    elif shift < 0:
+        tiles = [jnp.where(lane >= LANES + shift, before, own) for own, before in zip(tiles, [edge] + tiles[:-1])]
+    else:
+        return tiles
+    return [pltpu.roll(tile, (-shift) % LANES, 1) for tile in tiles]
+
+
+def plan_kernel(offsets, pair_epochs, pair_slot, inverse, lengths, table):
+    count = pair_slot.shape[0]
+    total = 2 * count
+    cells = SPAN * SPAN
+
+    ends = [pair_epochs[pair_slot[j], 0] for j in range(count)]
+    ends += [pair_epochs[pair_slot[j], 1] for j in range(count)]
+    ranks = [jnp.int32(0)] * total
+    for a in range(total):
+        for b in range(a + 1, total):
+            ahead = (ends[a] <= ends[b]).astype(jnp.int32)
+            ranks[b] = ranks[b] + ahead
+            ranks[a] = ranks[a] + (1 - ahead)
+    for a in range(total):
+        table[a] = ranks[a]
+        table[total + ranks[a]] = a
+        table[2 * total + ranks[a]] = ends[a]
+    for s in range(total - 1):
+        width = (table[2 * total + s + 1] - table[2 * total + s]).astype(jnp.float32)
+        lengths[s] = jnp.full((SUBLANES, LANES), width)
+
+    gram = [[None] * count for _ in range(count)]
+    for a in range(count):
+        for b in range(a, count):
+            shared = jnp.minimum(ends[count + a], ends[count + b]) - jnp.maximum(ends[a], ends[b])
+            value = jnp.maximum(shared, 0).astype(jnp.float32) + (PENALTY if a == b else 0.0)
+            gram[a][b] = gram[b][a] = jnp.full((SUBLANES, LANES), value)
+    for k in range(count):
+        pivot = 1.0 / gram[k][k]
+        scaled = [gram[k][b] * pivot for b in range(count)]
+        for a in range(count):
+            if a == k:
+                continue
+            factor = gram[a][k]
+            for b in range(count):
+                if b != k:
+                    gram[a][b] = gram[a][b] - factor * scaled[b]
+            gram[a][k] = -(factor * pivot)
+        for b in range(count):
+            gram[k][b] = scaled[b]
+        gram[k][k] = pivot
+    for a in range(count):
+        for b in range(count):
+            inverse[a * count + b] = gram[a][b]
+
+    first = 3 * total
+    listed = first + cells - offsets.shape[0]
+
+    def blank(cell, carry):
+        table[listed + cell] = 0
+        return carry
+
+    lax.fori_loop(0, cells, blank, 0, unroll=9)
+
+    def mark(k, carry):
+        cell = (offsets[k, 1] + SEARCH) * SPAN + offsets[k, 0] + SEARCH
+        table[listed + cell] = 1
+        return carry
+
+    lax.fori_loop(0, offsets.shape[0], mark, 0, unroll=8)
+
+    def collect(cell, place):
+        held = table[listed + cell]
+
+        @pl.when(held == 0)
+        def _():
+            table[first + place] = cell
+
+        return place + 1 - held
+
+    lax.fori_loop(0, cells, collect, 0, unroll=3)
+
+
+def prefix(lengths, values, running):
+    total = jnp.zeros((SUBLANES, LANES), jnp.float32)
+    running[0] = total
+    for s, value in enumerate(values):
+        total = total + lengths[s] * value
+        running[s + 1] = total
+
+
+def invert(count, group, fresh, observed, inverse, lengths, plan, sparse, spread, running, steps):
+    segments = 2 * count - 1
+    threshold = SPARSITY / PENALTY
+    residual = [observed[pl.ds(group * SUBLANES * SUBLANES + j, SUBLANES, stride=SUBLANES), :] for j in range(count)]
+    if not fresh:
+        prefix(lengths, [spread[s] for s in range(segments)], running)
+        residual = [
+            residual[j] - (running[plan[count + j]] - running[plan[j]]) for j in range(count)
+        ]
+    for a in range(count):
+        step = inverse[a * count] * residual[0]
+        for b in range(1, count):
+            step = step + inverse[a * count + b] * residual[b]
+        steps[a] = step
+        steps[count + a] = -step
+    level = None
+    for s in range(segments):
+        rise = steps[plan[2 * count + s]]
+        level = rise if level is None else level + rise
+        blended = level if fresh else sparse[s + 1] + level
+        scaled = jnp.clip(blended, -threshold, threshold)
+        shrunk = blended - scaled
+        sparse[s + 1] = shrunk
+        spread[s] = shrunk - scaled
+
+
+def invert_round(count, fresh, observed, inverse, lengths, plan, sparse, spread, running, steps):
+    groups = len(running)
+
+    def iterate(first):
+        for group in range(groups):
+            invert(
+                count,
+                group,
+                first,
+                observed,
+                inverse,
+                lengths,
+                plan,
+                sparse.at[group],
+                spread.at[group],
+                running[group],
+                steps[group],
+            )
+
+    if fresh:
+        iterate(True)
+
+    def later(iteration, carry):
+        iterate(False)
+        return carry
+
+    lax.fori_loop(1 if fresh else 0, ITERS, later, 0)
+
+
+def velocity_kernel(matched, sparse_in, spread_in, inverse, lengths, plan, velocity, sparse, spread, *buffers):
+    groups, held = sparse_in.shape[:2]
+    segments = held - 2
+    count = (segments + 1) // 2
+    halves = groups // 2
+    running, steps = buffers[:groups], buffers[groups:]
+    bounds = 4 * count
+    for group in range(groups):
+        sparse[group] = sparse_in[group]
+        spread[group] = spread_in[group]
+    invert_round(count, False, matched, inverse, lengths, plan, sparse, spread, running, steps)
+
+    def fill(low, high, s):
+        values = [sparse[group, s] for group in range(groups)]
+
+        def one(epoch, carry):
+            for group in range(groups):
+                half = group % halves
+                velocity[group // halves, epoch, half * SUBLANES : (half + 1) * SUBLANES, :] = values[group]
+            return carry
+
+        lax.fori_loop(low, high, one, 0)
+
+    fill(0, plan[bounds], 0)
+    for s in range(segments):
+        fill(plan[bounds + s], plan[bounds + s + 1], s + 1)
+    fill(plan[bounds + segments], velocity.shape[1], segments + 1)
+
+
+def signed_sums(terms):
+    total = terms[SEARCH]
+    moment = step = None
+    for distance in range(SEARCH, 0, -1):
+        below, above = terms[SEARCH - distance], terms[SEARCH + distance]
+        total = total + (above + below)
+        rise = above - below
+        step = rise if step is None else step + rise
+        moment = step if moment is None else moment + step
+    return total, moment
+
+
+def match(cells, first_guess, prior, predicted, table, matched):
+    def pixel_tile(cell, carry):
+        factors = []
+        for component in range(2):
+            value = prior[component * cells + cell]
+            if not first_guess:
+                at = pl.multiple_of((component * cells + cell) * SUBLANES, SUBLANES)
+                value = 0.5 * (value + predicted[pl.ds(at, SUBLANES), :])
+            nearest = jnp.clip(jnp.round(value), -float(SEARCH), float(SEARCH))
+            peak = nearest * value - 0.5 * nearest * nearest
+            factors.append(
+                [
+                    jnp.exp(value * float(shift) - (peak + 0.5 * shift * shift))
+                    for shift in range(-SEARCH, SEARCH + 1)
+                ]
+            )
+        weights, moments = [], []
+        for column_shift in range(SPAN):
+            total, moment = signed_sums(
+                [
+                    factors[0][row_shift] * table[(column_shift * SPAN + row_shift) * cells + cell]
+                    for row_shift in range(SPAN)
+                ]
+            )
+            weights.append(total * factors[1][column_shift])
+            moments.append(moment * factors[1][column_shift])
+        weight, column_moment = signed_sums(weights)
+        row_moment = moments[0]
+        for moment in moments[1:]:
+            row_moment = row_moment + moment
+        share = 1.0 / weight
+        for component, value in enumerate((row_moment, column_moment)):
+            at = pl.multiple_of((component * cells + cell) * SUBLANES, SUBLANES)
+            matched[pl.ds(at, SUBLANES), :] = value * share
+        return carry
+
+    lax.fori_loop(0, cells, pixel_tile, 0)
+
+
+def track_kernel(
+    offsets,
+    data,
+    inverse,
+    lengths,
+    plan,
+    motion,
+    matched,
+    sparse,
+    spread,
+    band,
+    first,
+    second,
+    mean_first,
+    scale_first,
+    mean_second,
+    scale_second,
+    table,
+    prior,
+    predicted,
+    *buffers,
+):
+    strip = SUBLANES
+    margin = SEARCH + RADIUS
+    tall = strip + 2 * RADIUS
+    taller = strip + 2 * margin
+    per = tall + taller + 2 * strip
+    wide = strip + 2 * SEARCH
+    area = float(WINDOW * WINDOW)
+    count = motion.shape[0]
+    columns = band.shape[1]
+    tiles = columns // LANES
+    cells = strip * tiles
+    groups = sparse.shape[0]
+    segments = 2 * count - 1
+    running, steps = buffers[:groups], buffers[groups:]
+    nothing = jnp.zeros((SUBLANES, LANES), jnp.float32)
+    lane = lax.broadcasted_iota(jnp.int32, (SUBLANES, LANES), 1)
+
+    tap = lax.broadcasted_iota(jnp.int32, band.shape[1:], 0)
+    column = lax.broadcasted_iota(jnp.int32, band.shape[1:], 1)
+    outside = jnp.where(column < LANES // 2, column + columns, column - LANES)
+    for place, centre in enumerate((column, jnp.where(column < LANES, outside, -columns))):
+        band[place] = jnp.where(jnp.abs(tap - centre) <= RADIUS, 1.0, 0.0).astype(jnp.bfloat16)
+
+    def fetch(row, tile):
+        return data[pl.ds(tile * per + row, SUBLANES, stride=tiles * per), :]
+
+    for component in range(2):
+        for row in range(strip):
+            for tile in range(tiles):
+                prior[component * cells + row * tiles + tile] = fetch(tall + taller + component * strip + row, tile)
+
+    images = [[fetch(row, tile) for row in range(tall)] for tile in range(tiles)]
+    for tile in range(tiles):
+        for row in range(tall):
+            first[row * tiles + tile] = images[tile][row]
+    chosen = [[fetch(tall + row, tile) for row in range(taller)] for tile in range(tiles)]
+
+    def multiply(columns_of_sums, totals, loads):
+        pieces = [[], [], []]
+        for sums in columns_of_sums:
+            split = [split_rows(sums[row], sums[row + 1]) for row in range(0, len(sums), 2)]
+            for part in range(3):
+                pieces[part].append(jnp.concatenate([parts[part] for parts in split], axis=0))
+        for part in range(3):
+            left = jnp.concatenate(pieces[part], axis=1)
+            for total, load in zip(totals, loads):
+                pltpu.matmul_acc_lhs(total, left, load_staged_rhs=load if part == 0 else None)
+
+    def statistics(*totals):
+        pltpu.matmul_push_rhs(band[0], 0, 0)
+        pltpu.matmul_push_rhs(band[1], 0, 1)
+        square = lambda field: [[row * row for row in rows] for rows in field]
+        sums_of = lambda field: [window_sums(rows) for rows in field]
+        for at, field in enumerate((images, square(images))):
+            multiply(sums_of(field), totals[at : at + 1], (0 if at == 0 else None,))
+        for at, field in enumerate((chosen, square(chosen))):
+            multiply(
+                sums_of(field), (totals[2 + at], totals[4 + at]), (None, 0 if at == 0 else None)
+            )
+        for row in range(taller):
+            pieces = [chosen[tile][row] for tile in range(tiles)]
+            for shift in range(-SEARCH, SEARCH + 1):
+                moved = lane_shift(pieces, nothing, shift, lane)
+                for tile in range(tiles):
+                    second[((shift + SEARCH) * taller + row) * tiles + tile] = moved[tile]
+        totals = [pltpu.matmul_pop(total) for total in totals]
+        for row in range(strip):
+            for tile in range(tiles):
+                at = (slice(row * SUBLANES, (row + 1) * SUBLANES), slice(tile * LANES, (tile + 1) * LANES))
+                mean = totals[0][at] / area
+                variance = totals[1][at] / area - mean * mean
+                mean_first[row * tiles + tile] = totals[0][at]
+                scale_first[row * tiles + tile] = lax.rsqrt(
+                    jnp.maximum(variance, VARIANCE_FLOOR)
+                ) * (SCALE / area)
+        for row in range(wide):
+            means, scales = [], []
+            rows = slice(row * SUBLANES, (row + 1) * SUBLANES)
+            for tile in range(tiles + 1):
+                source = 2 if tile < tiles else 4
+                lanes = slice(tile % tiles * LANES, (tile % tiles + 1) * LANES)
+                mean = totals[source][rows, lanes] / area
+                variance = totals[source + 1][rows, lanes] / area - mean * mean
+                means.append(mean)
+                scales.append(lax.rsqrt(jnp.maximum(variance, VARIANCE_FLOOR)))
+            for shift in range(-SEARCH, SEARCH + 1):
+                for values, held in ((means, mean_second), (scales, scale_second)):
+                    moved = lane_shift(values[:tiles], values[tiles], shift, lane)
+                    for tile in range(tiles):
+                        held[((shift + SEARCH) * wide + row) * tiles + tile] = moved[tile]
+
+    pl.run_scoped(
+        statistics,
+        *[
+            pltpu.ACC(unit)((rows * SUBLANES, columns), jnp.float32)
+            for unit, rows in ((0, strip), (0, strip), (0, wide), (0, wide), (1, wide), (1, wide))
+        ],
+    )
+
+    def clear(index, carry):
+        at = plan[6 * count + index] * cells
+        for cell in range(cells):
+            table[at + cell] = nothing
+        return carry
+
+    lax.fori_loop(0, SPAN * SPAN - offsets.shape[0], clear, 0)
+
+    def place(k):
+        return offsets[k, 0] + SEARCH, offsets[k, 1] + SEARCH
+
+    def send(k, total, load):
+        row_shift, column_shift = place(k)
+        at_second = (column_shift * taller + row_shift) * tiles
+        fields = []
+        for tile in range(tiles):
+            fields.append(
+                window_sums(
+                    [first[row * tiles + tile] * second[at_second + row * tiles + tile] for row in range(tall)]
+                )
+            )
+        multiply(fields, (total,), (load,))
+
+    def receive(k, total):
+        row_shift, column_shift = place(k)
+        at_second = (column_shift * wide + row_shift) * tiles
+        at_table = (column_shift * SPAN + row_shift) * cells
+        crossed = pltpu.matmul_pop(total)
+        for row in range(strip):
+            for tile in range(tiles):
+                cell = row * tiles + tile
+                value = crossed[row * SUBLANES : (row + 1) * SUBLANES, tile * LANES : (tile + 1) * LANES]
+                covariance = value - mean_first[cell] * mean_second[at_second + cell]
+                scaled = covariance * (scale_first[cell] * scale_second[at_second + cell])
+                table[at_table + cell] = jnp.exp2(scaled)
+
+    def all_offsets(*totals):
+        pltpu.matmul_push_rhs(band[0], 0, 1)
+        for member in range(GROUP):
+            send(member, totals[member], 0 if member == 1 else None)
+
+        def offset_group(group, carry):
+            for member in range(GROUP):
+                receive((group - 1) * GROUP + member, totals[member])
+                send(group * GROUP + member, totals[member], None)
+            return carry
+
+        lax.fori_loop(1, offsets.shape[0] // GROUP, offset_group, 0)
+        for member in range(GROUP):
+            receive(offsets.shape[0] - GROUP + member, totals[member])
+
+    pl.run_scoped(
+        all_offsets,
+        *[pltpu.ACC(member % 2)((strip * SUBLANES, columns), jnp.float32) for member in range(GROUP)],
+    )
+
+    for group in range(groups):
+        sparse[group, 0] = nothing
+        sparse[group, segments + 1] = nothing
+    match(cells, True, prior, predicted, table, matched)
+    for round_number in range(1, ROUNDS):
+        invert_round(
+            count, round_number == 1, matched, inverse, lengths, plan, sparse, spread, running, steps
+        )
+        for group in range(groups):
+            prefix(lengths, [sparse[group, s + 1] for s in range(segments)], running[group])
+            for j in range(count):
+                predicted[pl.ds(group * SUBLANES * SUBLANES + j, SUBLANES, stride=SUBLANES), :] = (
+                    running[group][plan[count + j]] - running[group][plan[j]]
+                )
+        match(cells, False, prior, predicted, table, matched)
+
+    for j in range(count):
+        for component in range(2):
+            for tile in range(tiles):
+                at = (component * cells + tile) * SUBLANES + j
+                motion[j, component, :, tile * LANES : (tile + 1) * LANES] = matched[
+                    pl.ds(at, SUBLANES, stride=tiles * SUBLANES), :
+                ]
+
+
+def by_strips(first_image, second_image, prior_motion, offsets, pair_epochs, pair_slot):
+    band_rows, columns = first_image.shape[1:]
+    margin = SEARCH + RADIUS
+    count = lax.axis_size("pairs")
+    strip = band_rows // count
+    tiles = columns // LANES
+    cells = strip * tiles
+    tall = strip + 2 * RADIUS
+    taller = strip + 2 * margin
+    wide = strip + 2 * SEARCH
+    per = tall + taller + 2 * strip
+    vmem_spec = pl.BlockSpec(memory_space=pltpu.VMEM)
+    images = (first_image[0], second_image[0])
+    others = [lax.ppermute(image, "rows", [(0, 1), (1, 0)]) for image in images]
+    message = (count * tiles * per, LANES)
+    sources = [pltpu.with_memory_space_constraint(x, pltpu.HBM) for x in (*images, prior_motion[:, 0])]
+    packed = pl.pallas_call(
+        pack_kernel,
+        out_shape=pltpu.VMEM(message, jnp.float32),
+        in_specs=[pl.BlockSpec(memory_space=pltpu.HBM)] * 3,
+        out_specs=vmem_spec,
+        scratch_shapes=[pltpu.VMEM(x.shape, jnp.float32) for x in sources] + [pltpu.SemaphoreType.DMA((3,))],
+        compiler_params=pltpu.CompilerParams(vmem_limit_bytes=4 * 1024 * 1024),
+    )(*sources)
+    packed = pl.pallas_call(
+        patch_kernel,
+        out_shape=pltpu.HBM(message, jnp.float32),
+        in_specs=[vmem_spec] * 3,
+        out_specs=pl.BlockSpec(memory_space=pltpu.HBM),
+        scratch_shapes=[
+            pltpu.VMEM((tiles * per, LANES), jnp.float32),
+            pltpu.SemaphoreType.DMA((3,)),
+        ],
+        compiler_params=pltpu.CompilerParams(vmem_limit_bytes=4 * 1024 * 1024),
+    )(*others, packed)
+    arrived = lax.all_to_all(packed, "pairs", split_axis=0, concat_axis=0, tiled=True)
+    tile = lambda *lead: pltpu.VMEM((*lead, SUBLANES, LANES), jnp.float32)
+    shape = lambda *lead: jax.ShapeDtypeStruct((*lead, SUBLANES, LANES), jnp.float32)
+    flat = jax.ShapeDtypeStruct((2 * cells * SUBLANES, LANES), jnp.float32)
+    groups = 2 * cells // SUBLANES
+    segments = 2 * count - 1
+    smem = pl.BlockSpec(memory_space=pltpu.SMEM)
+    vmem = pl.BlockSpec(memory_space=pltpu.VMEM)
+    buffers = [tile(2 * count)] * groups + [tile(2 * count)] * groups
+    entries = 6 * count + 2 * SPAN * SPAN - offsets.shape[0]
+    inverse, lengths, plan = pl.pallas_call(
+        plan_kernel,
+        out_shape=(
+            shape(count * count),
+            shape(segments),
+            jax.ShapeDtypeStruct((entries,), jnp.int32),
+        ),
+        in_specs=[smem] * 3,
+        out_specs=(vmem, vmem, smem),
+        compiler_params=pltpu.CompilerParams(vmem_limit_bytes=4 * 1024 * 1024),
+    )(offsets, pair_epochs, pair_slot)
+    motion, matched, sparse, spread = pl.pallas_call(
+        track_kernel,
+        out_shape=(
+            jax.ShapeDtypeStruct((count, 2, strip, columns), jnp.float32),
+            flat,
+            shape(groups, segments + 2),
+            shape(groups, segments),
+        ),
+        in_specs=[smem, vmem, vmem, vmem, smem],
+        out_specs=(vmem, vmem, vmem, vmem),
+        scratch_shapes=[
+            pltpu.VMEM((2, columns, columns), jnp.bfloat16),
+            tile(tall * tiles),
+            tile(SPAN * taller * tiles),
+            tile(cells),
+            tile(cells),
+            tile(SPAN * wide * tiles),
+            tile(SPAN * wide * tiles),
+            tile(SPAN * SPAN * cells),
+            tile(2 * cells),
+            pltpu.VMEM(flat.shape, jnp.float32),
+            *buffers,
+        ],
+        compiler_params=pltpu.CompilerParams(vmem_limit_bytes=32 * 1024 * 1024),
+    )(offsets, arrived, inverse, lengths, plan)
+    velocity = pl.pallas_call(
+        velocity_kernel,
+        out_shape=jax.ShapeDtypeStruct((2, EPOCHS, cells, LANES), jnp.float32),
+        in_specs=[vmem] * 5 + [smem],
+        out_specs=vmem,
+        scratch_shapes=[tile(groups, segments + 2), tile(groups, segments), *buffers],
+        compiler_params=pltpu.CompilerParams(vmem_limit_bytes=16 * 1024 * 1024),
+    )(matched, sparse, spread, inverse, lengths, plan)
+    returned = lax.all_to_all(motion, "pairs", split_axis=0, concat_axis=0, tiled=True)
+    returned = jnp.moveaxis(returned, 0, 1).reshape(2, 1, band_rows, columns)
+    return (velocity.reshape(2, EPOCHS, 1, strip * columns), returned)
+
+
+def per_device_any(first_image, second_image, *rest):
+    band_rows, columns = first_image.shape[1:]
+    count = lax.axis_size("pairs")
+    strips = (
+        count == SUBLANES
+        and band_rows == count * SUBLANES
+        and columns == 2 * LANES
+        and lax.axis_size("rows") == 2
+        and rest[1].shape[0] % GROUP == 0
+    )
+    plan = by_strips if strips else per_device
+    return plan(first_image, second_image, *rest)
+
+
 def solution(mesh):
     placed = (
         P(("groups", "pairs"), "rows", None),
@@ -195,7 +839,7 @@
         P("groups"),
     )
     return jax.shard_map(
-        per_device,
+        per_device_any,
         mesh=mesh,
         in_specs=placed,
         out_specs=(

time: 898 us -> 45.8 us (0.05); the launches traced: 884 us -> 45.5 us
  local copies, waits for them, and re-layouts: 749 us -> 0.85 us
  other arithmetic: 38.3 us -> 0 us
  matrix products: 35.7 us -> 0 us
  Pallas kernels: 0 us -> 18.1 us
  starting transfers between devices: 27.1 us -> 11.2 us
  loops' own time: 10.8 us -> 0 us
    gather x1152 -> x0, local copies, waits for them, and re-layouts: 739 us -> none
    dot_general x76 -> x0, matrix products: 35.7 us -> none  [the longest x8 16.9 us: per_device(): jnp.einsum('ef,cfn->cen', inverse_matrix, target, precision=HIGHEST)]
    reduce_max x17 -> x0, other arithmetic: 19.4 us -> none  [the longest x16 18.8 us: block_step(): new_max = jnp.maximum(running_max, jnp.max(match_scores, axis=0))]
    pallas_call x0 -> x5, Pallas kernels: none -> 18.1 us  [the longest x1 9.84 us: by_strips(): pl.pallas_call(track_kernel, out_shape=(jax.ShapeDtypeStruct((count, 2, s...]
    all_to_all x3 -> x2, starting transfers between devices: 23.4 us -> 10.6 us  [the longest x1 6.96 us: by_strips(): lax.all_to_all(packed, 'pairs', split_axis=0, concat_axis=0, tiled=True)]
    another operation x50 -> x0, loops' own time: 10.8 us -> none  [the longest x16 3.01 us: correlate(): lax.dynamic_slice(second_padded, (row_start, col_start), (height + 2 * RA...]
    add x35 -> x0, other arithmetic: 10.5 us -> none  [the longest x19 9.5 us: box_sum(): running = running + values[..., position:position + height, :]]
    all_to_all x3 -> x2, waiting for transfers between devices: 21.4 us -> 14.3 us  [the longest x1 10.5 us: by_strips(): lax.all_to_all(packed, 'pairs', split_axis=0, concat_axis=0, tiled=True)]
  transfers between devices with their start and end apart: 5 -> 4, of which waited for: 3 -> 3; matrix products, arithmetic and copies ran while one was open for 2% -> 0% of each run, Pallas kernels for 0% -> 16%
where the time goes in v2:
time: 45.8 us; the launch traced here: 45.5 us
  Pallas kernels  18.1 us (40%)
  waiting for transfers between devices  14.7 us (32%)
  starting transfers between devices  11.2 us (24%)
  local copies, waits for them, and re-layouts  0.85 us (2%)
  between operations  0.69 us (2%)
    all_to_all x1, waiting for transfers between devices, by_strips(): lax.all_to_all(packed, 'pairs', split_axis=0, concat_axis=0, tiled=True)  10.5 us
    pallas_call x1, Pallas kernels, by_strips(): pl.pallas_call(track_kernel, out_shape=(jax.ShapeDtypeStruct((count, 2, s...  9.84 us
    all_to_all x1, starting transfers between devices, by_strips(): lax.all_to_all(packed, 'pairs', split_axis=0, concat_axis=0, tiled=True)  6.96 us
    all_to_all x1, waiting for transfers between devices, by_strips(): lax.all_to_all(motion, 'pairs', split_axis=0, concat_axis=0, tiled=True)  3.79 us
    all_to_all x1, starting transfers between devices, by_strips(): lax.all_to_all(motion, 'pairs', split_axis=0, concat_axis=0, tiled=True)  3.63 us
    pallas_call x1, Pallas kernels, by_strips(): pl.pallas_call(velocity_kernel, out_shape=jax.ShapeDtypeStruct((2, EPOCHS...  3.55 us
    pallas_call x1, Pallas kernels, by_strips(): pl.pallas_call(plan_kernel, out_shape=(shape(count * count), shape(segmen...  2.88 us
    pallas_call x1, Pallas kernels, by_strips(): pl.pallas_call(pack_kernel, out_shape=pltpu.VMEM(message, jnp.float32), i...  1.01 us
  transfers between devices with their start and end apart: 4, of which 3 were waited for; matrix products, arithmetic and copies ran while one was open for 0% of the time, Pallas kernels for 16%

profile of v2, /device:TPU:0, one launch (start us, length us, event | category | flops | bytes accessed | tf_op | source)
XLA Modules:
  0.0 45.5 jit_solution(2639641882353219881)
XLA Ops:
  0.6 0.0 copy-start.1
  0.6 0.0 copy-start.2
  0.7 0.0 copy-start
  0.7 0.6 %collective-permute-start = (f32[64,256]{1,0:T(8,128)}, f32[64,256]{1,0:T(8,128)S(1)}, u32[]{:S(2)}, u32[]{:S(2)}) collective-permute-start(f32[64,256]{1,0:T(8,128)} %bitcast.17), channel_id=1, source_target_pairs={{0,1},{1,0},{2,3},{3,2},{4,5},{5,4},{6,7},{7,6},{8,9},{9,8},{10,11... | collective-permute-start | bytes 196616 | tf_op jit(solution)/shard_map/ppermute | solution.py:737
  1.2 0.1 collective-permute-start.1
  1.3 1.0 %shard_map.77.packed = f32[896,128]{1,0:T(8,128)S(1)} custom-call(f32[64,256]{1,0:T(8,128)} %bitcast.18, f32[64,256]{1,0:T(8,128)} %bitcast.20, f32[2,64,256]{2,1,0:T(8,128)} %bitcast.16), custom_call_target="tpu_custom_call" | custom-call | tf_op jit(solution)/shard_map/pallas_call | solution.py:740
  2.3 0.0 collective-permute-done.other_first
  2.3 0.4 collective-permute-done.1.other_second
  2.7 0.8 %shard_map.78 = f32[896,128]{1,0:T(8,128)} custom-call(f32[64,256]{1,0:T(8,128)S(1)} %collective-permute-done.other_first, f32[64,256]{1,0:T(8,128)S(1)} %collective-permute-done.1.other_second, f32[896,128]{1,0:T(8,128)S(1)} %shard_map.77.packed), custom_call_target="tpu_custom_call" | custom-call | tf_op jit(solution)/shard_map/pallas_call | solution.py:748
  3.5 7.0 %all-to-all-start = ((f32[8,112,128]{2,1,0:T(8,128)}), f32[8,112,128]{2,1,0:T(8,128)S(1)}, u32[]{:S(2)}, u32[]{:S(2)}) async-start(f32[8,112,128]{2,1,0:T(8,128)} %bitcast.15), calls=%async_computation | async-start | bytes 917504 | tf_op jit(solution)/shard_map/all_to_all | solution.py:759
  10.4 0.0 copy-done.1
  10.4 0.1 copy.13.pair_epochs
  10.5 0.0 copy-done.2
  10.5 0.1 copy.14.offsets
  10.6 0.0 copy-done
  10.6 2.9 %shard_map.79 = (f32[64,8,128]{2,1,0:T(8,128)S(1)}, f32[15,8,128]{2,1,0:T(8,128)S(1)}, s32[146]{0:T(256)S(1)}) custom-call(s32[64,2]{1,0:T(8,128)S(1)} %copy.14.offsets, s32[8,2]{1,0:T(8,128)S(1)} %copy.13.pair_epochs, s32[8]{0:T(128)S(1)} %copy-done), custom_call_target="tpu_custom_call" | custom-call | tf_op jit(solution)/shard_map/pallas_call | solution.py:769
  13.5 10.5 %all-to-all-done = f32[8,112,128]{2,1,0:T(8,128)S(1)} async-done(((f32[8,112,128]{2,1,0:T(8,128)}), f32[8,112,128]{2,1,0:T(8,128)S(1)}, u32[]{:S(2)}, u32[]{:S(2)}) %all-to-all-start) | async-done | bytes 458784 | tf_op jit(solution)/shard_map/all_to_all | solution.py:759
  24.0 9.8 %shard_map.80 = (f32[8,2,8,256]{3,2,1,0:T(8,128)}, f32[256,128]{1,0:T(8,128)S(1)}, f32[4,17,8,128]{3,2,1,0:T(8,128)S(1)}, f32[4,15,8,128]{3,2,1,0:T(8,128)S(1)}) custom-call(s32[64,2]{1,0:T(8,128)S(1)} %copy.14.offsets, f32[896,128]{1,0:T(8,128)S(1)} %bitcast.13, f32[64,8,128]{2,1,0:T(8,128)S(1)} %get-tuple-element.9.inverse, ...), custom_call_target="tpu_custom_call" | custom-call | tf_op jit(solution)/shard_map/pallas_call | solution.py:780
  33.9 3.6 %all-to-all-start.1 = ((f32[8,2,8,256]{3,2,1,0:T(8,128)}), f32[8,2,8,256]{3,2,1,0:T(8,128)S(1)}, u32[]{:S(2)}, u32[]{:S(2)}) async-start(f32[8,2,8,256]{3,2,1,0:T(8,128)} %get-tuple-element.15), calls=%async_computation.1 | async-start | bytes 262144 | tf_op jit(solution)/shard_map/all_to_all | solution.py:813
  37.5 3.5 %shard_map.81 = f32[2,128,16,128]{3,2,1,0:T(8,128)} custom-call(f32[256,128]{1,0:T(8,128)S(1)} %get-tuple-element.12.matched, f32[4,17,8,128]{3,2,1,0:T(8,128)S(1)} %get-tuple-element.13.sparse_in, f32[4,15,8,128]{3,2,1,0:T(8,128)S(1)} %get-tuple-element.14.spread_in, f32[64,8,128]{2,1,0:T(8,128)S(1)} %get-tuple-element.9.inverse, ...), custom_call_target="tpu_custom_call" | custom-call | tf_op jit(solution)/shard_map/pallas_call | solution.py:805
  41.1 3.8 %all-to-all-done.1 = f32[8,2,8,256]{3,2,1,0:T(8,128)S(1)} async-done(((f32[8,2,8,256]{3,2,1,0:T(8,128)}), f32[8,2,8,256]{3,2,1,0:T(8,128)S(1)}, u32[]{:S(2)}, u32[]{:S(2)}) %all-to-all-start.1) | async-done | bytes 131104 | tf_op jit(solution)/shard_map/all_to_all | solution.py:813
  44.9 0.7 %copy_bitcast_fusion = f32[2,1,64,256]{3,2,1,0:T(8,128)} fusion(f32[8,2,8,256]{3,2,1,0:T(8,128)S(1)} %all-to-all-done.1), kind=kLoop, calls=%fused_computation | loop fusion | bytes 262144
Async XLA Ops:
  0.6 9.8 %copy-start.1 = (s32[8,2]{0,1:T(2,128)S(1)}, s32[8,2]{0,1:T(2,128)}, u32[]{:S(2)}) copy-start(s32[8,2]{0,1:T(2,128)} %param.10) | copy-start | bytes 196
  0.6 9.9 %copy-start.2 = (s32[64,2]{0,1:T(2,128)S(1)}, s32[64,2]{0,1:T(2,128)}, u32[]{:S(2)}) copy-start(s32[64,2]{0,1:T(2,128)} %param.9) | copy-start | bytes 1540
  0.7 10.0 %copy-start = (s32[8]{0:T(128)S(1)}, s32[8]{0:T(128)}, u32[]{:S(2)}) copy-start(s32[8]{0:T(128)} %pair_slot.1) | copy-start | bytes 100
  0.7 1.7 %collective-permute-start = (f32[64,256]{1,0:T(8,128)}, f32[64,256]{1,0:T(8,128)S(1)}, u32[]{:S(2)}, u32[]{:S(2)}) collective-permute-start(f32[64,256]{1,0:T(8,128)} %bitcast.17), channel_id=1, source_target_pairs={{0,1},{1,0},{2,3},{3,2},{4,5},{5,4},{6,7},{7,6},{8,9},{9,8},{10,11... | collective-permute-start | bytes 196616 | tf_op jit(solution)/shard_map/ppermute | solution.py:737
  1.2 1.5 %collective-permute-start.1 = (f32[64,256]{1,0:T(8,128)}, f32[64,256]{1,0:T(8,128)S(1)}, u32[]{:S(2)}, u32[]{:S(2)}) collective-permute-start(f32[64,256]{1,0:T(8,128)} %bitcast.19), channel_id=1, source_target_pairs={{0,1},{1,0},{2,3},{3,2},{4,5},{5,4},{6,7},{7,6},{8,9},{9,8},{10,11... | collective-permute-start | bytes 196616 | tf_op jit(solution)/shard_map/ppermute | solution.py:737
  3.5 20.6 %all-to-all-start = ((f32[8,112,128]{2,1,0:T(8,128)}), f32[8,112,128]{2,1,0:T(8,128)S(1)}, u32[]{:S(2)}, u32[]{:S(2)}) async-start(f32[8,112,128]{2,1,0:T(8,128)} %bitcast.15), calls=%async_computation | async-start | bytes 917504 | tf_op jit(solution)/shard_map/all_to_all | solution.py:759
  33.9 11.0 %all-to-all-start.1 = ((f32[8,2,8,256]{3,2,1,0:T(8,128)}), f32[8,2,8,256]{3,2,1,0:T(8,128)S(1)}, u32[]{:S(2)}, u32[]{:S(2)}) async-start(f32[8,2,8,256]{3,2,1,0:T(8,128)} %get-tuple-element.15), calls=%async_computation.1 | async-start | bytes 262144 | tf_op jit(solution)/shard_map/all_to_all | solution.py:813

commit v3 on v2

--- a/solution.py
+++ b/solution.py
@@ -191,10 +191,11 @@
 
 LANES = 128
 SUBLANES = 8
-GROUP = 4
+GROUP = 16
 SPAN = 2 * SEARCH + 1
 WINDOW = 2 * RADIUS + 1
-SCALE = 1.4426950408889634 / SOFTMIN_HEAT
+LOG2E = 1.4426950408889634
+SCALE = LOG2E / SOFTMIN_HEAT
 
 
 def strip_rows(strip):
@@ -277,11 +278,19 @@
 
 
 def window_sums(rows):
-    count = len(rows)
-    twos = [rows[a] + rows[a + 1] for a in range(count - 1)]
-    fours = [twos[a] + twos[a + 2] for a in range(count - 3)]
-    eights = [fours[a] + fours[a + 4] for a in range(count - 7)]
-    return [eights[a] + rows[a + 8] for a in range(count - 8)]
+    sums = []
+    for top in range(0, len(rows) - WINDOW + 1, WINDOW - 1):
+        size = min(WINDOW - 1, len(rows) - WINDOW + 1 - top)
+        before = [rows[top + WINDOW - 2]]
+        for row in range(WINDOW - 3, -1, -1):
+            before.append(rows[top + row] + before[-1])
+        before.reverse()
+        after = rows[top + WINDOW - 1]
+        for row in range(size):
+            sums.append(before[row] + after)
+            if row + 1 < size:
+                after = after + rows[top + WINDOW + row]
+    return sums
 
 
 def split_rows(upper, lower):
@@ -436,7 +445,7 @@
         iterate(False)
         return carry
 
-    lax.fori_loop(1 if fresh else 0, ITERS, later, 0)
+    lax.fori_loop(1 if fresh else 0, ITERS, later, 0, unroll=True)
 
 
 def velocity_kernel(matched, sparse_in, spread_in, inverse, lengths, plan, velocity, sparse, spread, *buffers):
@@ -489,13 +498,15 @@
                 at = pl.multiple_of((component * cells + cell) * SUBLANES, SUBLANES)
                 value = 0.5 * (value + predicted[pl.ds(at, SUBLANES), :])
             nearest = jnp.clip(jnp.round(value), -float(SEARCH), float(SEARCH))
-            peak = nearest * value - 0.5 * nearest * nearest
-            factors.append(
-                [
-                    jnp.exp(value * float(shift) - (peak + 0.5 * shift * shift))
-                    for shift in range(-SEARCH, SEARCH + 1)
-                ]
-            )
+            centre = nearest * (0.5 * LOG2E * nearest - LOG2E * value)
+            slope = LOG2E * value
+            powers = {0: jnp.exp2(centre)}
+            for shift in range(1, SEARCH + 1):
+                level = centre - 0.5 * LOG2E * shift * shift
+                rise = slope * float(shift)
+                powers[shift] = jnp.exp2(level + rise)
+                powers[-shift] = jnp.exp2(level - rise)
+            factors.append([powers[shift] for shift in range(-SEARCH, SEARCH + 1)])
         weights, moments = [], []
         for column_shift in range(SPAN):
             total, moment = signed_sums(
@@ -516,7 +527,7 @@
             matched[pl.ds(at, SUBLANES), :] = value * share
         return carry
 
-    lax.fori_loop(0, cells, pixel_tile, 0)
+    lax.fori_loop(0, cells, pixel_tile, 0, unroll=2)
 
 
 def track_kernel(
@@ -557,6 +568,14 @@
     running, steps = buffers[:groups], buffers[groups:]
     nothing = jnp.zeros((SUBLANES, LANES), jnp.float32)
     lane = lax.broadcasted_iota(jnp.int32, (SUBLANES, LANES), 1)
+
+    def clear(index, carry):
+        at = plan[6 * count + index] * cells
+        for cell in range(cells):
+            table[at + cell] = nothing
+        return carry
+
+    lax.fori_loop(0, SPAN * SPAN - offsets.shape[0], clear, 0)
 
     tap = lax.broadcasted_iota(jnp.int32, band.shape[1:], 0)
     column = lax.broadcasted_iota(jnp.int32, band.shape[1:], 1)
@@ -639,14 +658,6 @@
             for unit, rows in ((0, strip), (0, strip), (0, wide), (0, wide), (1, wide), (1, wide))
         ],
     )
-
-    def clear(index, carry):
-        at = plan[6 * count + index] * cells
-        for cell in range(cells):
-            table[at + cell] = nothing
-        return carry
-
-    lax.fori_loop(0, SPAN * SPAN - offsets.shape[0], clear, 0)
 
     def place(k):
         return offsets[k, 0] + SEARCH, offsets[k, 1] + SEARCH

time: 45.8 us -> 44.4 us (0.969)
  Pallas kernels: 18.1 us -> 16.6 us
    pallas_call x1, Pallas kernels: 9.84 us -> 8.46 us  [by_strips(): pl.pallas_call(track_kernel, out_shape=(jax.ShapeDtypeStruct((count, 2, s...]
  transfers between devices with their start and end apart: 4 -> 4, of which waited for: 3 -> 3; matrix products, arithmetic and copies ran while one was open for 0% -> 0% of each run, Pallas kernels for 16% -> 17%
where the time goes in v3:
time: 44.4 us; the launch traced here: 44.2 us
  Pallas kernels  16.6 us (37%)
  waiting for transfers between devices  14.8 us (33%)
  starting transfers between devices  11.2 us (25%)
  local copies, waits for them, and re-layouts  0.85 us (2%)
  between operations  0.69 us (2%)
    all_to_all x1, waiting for transfers between devices, by_strips(): lax.all_to_all(packed, 'pairs', split_axis=0, concat_axis=0, tiled=True)  10.5 us
    pallas_call x1, Pallas kernels, by_strips(): pl.pallas_call(track_kernel, out_shape=(jax.ShapeDtypeStruct((count, 2, s...  8.46 us
    all_to_all x1, starting transfers between devices, by_strips(): lax.all_to_all(packed, 'pairs', split_axis=0, concat_axis=0, tiled=True)  6.96 us
    all_to_all x1, waiting for transfers between devices, by_strips(): lax.all_to_all(motion, 'pairs', split_axis=0, concat_axis=0, tiled=True)  3.9 us
    all_to_all x1, starting transfers between devices, by_strips(): lax.all_to_all(motion, 'pairs', split_axis=0, concat_axis=0, tiled=True)  3.65 us
    pallas_call x1, Pallas kernels, by_strips(): pl.pallas_call(velocity_kernel, out_shape=jax.ShapeDtypeStruct((2, EPOCHS...  3.45 us
    pallas_call x1, Pallas kernels, by_strips(): pl.pallas_call(plan_kernel, out_shape=(shape(count * count), shape(segmen...  2.88 us
    pallas_call x1, Pallas kernels, by_strips(): pl.pallas_call(pack_kernel, out_shape=pltpu.VMEM(message, jnp.float32), i...  1.01 us
  transfers between devices with their start and end apart: 4, of which 3 were waited for; matrix products, arithmetic and copies ran while one was open for 0% of the time, Pallas kernels for 17%

profile of v3, /device:TPU:0, one launch (start us, length us, event | category | flops | bytes accessed | tf_op | source)
XLA Modules:
  0.0 44.2 jit_solution(11098455692264741810)
XLA Ops:
  0.6 0.0 copy-start.1
  0.6 0.0 copy-start.2
  0.7 0.0 copy-start
  0.7 0.6 %collective-permute-start = (f32[64,256]{1,0:T(8,128)}, f32[64,256]{1,0:T(8,128)S(1)}, u32[]{:S(2)}, u32[]{:S(2)}) collective-permute-start(f32[64,256]{1,0:T(8,128)} %bitcast.17), channel_id=1, source_target_pairs={{0,1},{1,0},{2,3},{3,2},{4,5},{5,4},{6,7},{7,6},{8,9},{9,8},{10,11... | collective-permute-start | bytes 196616 | tf_op jit(solution)/shard_map/ppermute | solution.py:748
  1.2 0.1 collective-permute-start.1
  1.3 1.0 %shard_map.77.packed = f32[896,128]{1,0:T(8,128)S(1)} custom-call(f32[64,256]{1,0:T(8,128)} %bitcast.18, f32[64,256]{1,0:T(8,128)} %bitcast.20, f32[2,64,256]{2,1,0:T(8,128)} %bitcast.16), custom_call_target="tpu_custom_call" | custom-call | tf_op jit(solution)/shard_map/pallas_call | solution.py:751
  2.3 0.0 collective-permute-done.other_first
  2.3 0.4 collective-permute-done.1.other_second
  2.7 0.8 %shard_map.78 = f32[896,128]{1,0:T(8,128)} custom-call(f32[64,256]{1,0:T(8,128)S(1)} %collective-permute-done.other_first, f32[64,256]{1,0:T(8,128)S(1)} %collective-permute-done.1.other_second, f32[896,128]{1,0:T(8,128)S(1)} %shard_map.77.packed), custom_call_target="tpu_custom_call" | custom-call | tf_op jit(solution)/shard_map/pallas_call | solution.py:759
  3.5 7.0 %all-to-all-start = ((f32[8,112,128]{2,1,0:T(8,128)}), f32[8,112,128]{2,1,0:T(8,128)S(1)}, u32[]{:S(2)}, u32[]{:S(2)}) async-start(f32[8,112,128]{2,1,0:T(8,128)} %bitcast.15), calls=%async_computation | async-start | bytes 917504 | tf_op jit(solution)/shard_map/all_to_all | solution.py:770
  10.4 0.0 copy-done.1
  10.4 0.1 copy.13.pair_epochs
  10.5 0.0 copy-done.2
  10.5 0.1 copy.14.offsets
  10.6 0.0 copy-done
  10.6 2.9 %shard_map.79 = (f32[64,8,128]{2,1,0:T(8,128)S(1)}, f32[15,8,128]{2,1,0:T(8,128)S(1)}, s32[146]{0:T(256)S(1)}) custom-call(s32[64,2]{1,0:T(8,128)S(1)} %copy.14.offsets, s32[8,2]{1,0:T(8,128)S(1)} %copy.13.pair_epochs, s32[8]{0:T(128)S(1)} %copy-done), custom_call_target="tpu_custom_call" | custom-call | tf_op jit(solution)/shard_map/pallas_call | solution.py:780
  13.5 10.5 %all-to-all-done = f32[8,112,128]{2,1,0:T(8,128)S(1)} async-done(((f32[8,112,128]{2,1,0:T(8,128)}), f32[8,112,128]{2,1,0:T(8,128)S(1)}, u32[]{:S(2)}, u32[]{:S(2)}) %all-to-all-start) | async-done | bytes 458784 | tf_op jit(solution)/shard_map/all_to_all | solution.py:770
  24.0 8.5 %shard_map.80 = (f32[8,2,8,256]{3,2,1,0:T(8,128)}, f32[256,128]{1,0:T(8,128)S(1)}, f32[4,17,8,128]{3,2,1,0:T(8,128)S(1)}, f32[4,15,8,128]{3,2,1,0:T(8,128)S(1)}) custom-call(s32[64,2]{1,0:T(8,128)S(1)} %copy.14.offsets, f32[896,128]{1,0:T(8,128)S(1)} %bitcast.13, f32[64,8,128]{2,1,0:T(8,128)S(1)} %get-tuple-element.9.inverse, ...), custom_call_target="tpu_custom_call" | custom-call | tf_op jit(solution)/shard_map/pallas_call | solution.py:791
  32.5 3.6 %all-to-all-start.1 = ((f32[8,2,8,256]{3,2,1,0:T(8,128)}), f32[8,2,8,256]{3,2,1,0:T(8,128)S(1)}, u32[]{:S(2)}, u32[]{:S(2)}) async-start(f32[8,2,8,256]{3,2,1,0:T(8,128)} %get-tuple-element.15), calls=%async_computation.1 | async-start | bytes 262144 | tf_op jit(solution)/shard_map/all_to_all | solution.py:824
  36.1 3.4 %shard_map.81 = f32[2,128,16,128]{3,2,1,0:T(8,128)} custom-call(f32[256,128]{1,0:T(8,128)S(1)} %get-tuple-element.12.matched, f32[4,17,8,128]{3,2,1,0:T(8,128)S(1)} %get-tuple-element.13.sparse_in, f32[4,15,8,128]{3,2,1,0:T(8,128)S(1)} %get-tuple-element.14.spread_in, f32[64,8,128]{2,1,0:T(8,128)S(1)} %get-tuple-element.9.inverse, ...), custom_call_target="tpu_custom_call" | custom-call | tf_op jit(solution)/shard_map/pallas_call | solution.py:816
  39.6 3.9 %all-to-all-done.1 = f32[8,2,8,256]{3,2,1,0:T(8,128)S(1)} async-done(((f32[8,2,8,256]{3,2,1,0:T(8,128)}), f32[8,2,8,256]{3,2,1,0:T(8,128)S(1)}, u32[]{:S(2)}, u32[]{:S(2)}) %all-to-all-start.1) | async-done | bytes 131104 | tf_op jit(solution)/shard_map/all_to_all | solution.py:824
  43.5 0.7 %copy_bitcast_fusion = f32[2,1,64,256]{3,2,1,0:T(8,128)} fusion(f32[8,2,8,256]{3,2,1,0:T(8,128)S(1)} %all-to-all-done.1), kind=kLoop, calls=%fused_computation | loop fusion | bytes 262144
Async XLA Ops:
  0.6 9.8 %copy-start.1 = (s32[8,2]{0,1:T(2,128)S(1)}, s32[8,2]{0,1:T(2,128)}, u32[]{:S(2)}) copy-start(s32[8,2]{0,1:T(2,128)} %param.10) | copy-start | bytes 196
  0.6 9.9 %copy-start.2 = (s32[64,2]{0,1:T(2,128)S(1)}, s32[64,2]{0,1:T(2,128)}, u32[]{:S(2)}) copy-start(s32[64,2]{0,1:T(2,128)} %param.9) | copy-start | bytes 1540
  0.7 10.0 %copy-start = (s32[8]{0:T(128)S(1)}, s32[8]{0:T(128)}, u32[]{:S(2)}) copy-start(s32[8]{0:T(128)} %pair_slot.1) | copy-start | bytes 100
  0.7 1.7 %collective-permute-start = (f32[64,256]{1,0:T(8,128)}, f32[64,256]{1,0:T(8,128)S(1)}, u32[]{:S(2)}, u32[]{:S(2)}) collective-permute-start(f32[64,256]{1,0:T(8,128)} %bitcast.17), channel_id=1, source_target_pairs={{0,1},{1,0},{2,3},{3,2},{4,5},{5,4},{6,7},{7,6},{8,9},{9,8},{10,11... | collective-permute-start | bytes 196616 | tf_op jit(solution)/shard_map/ppermute | solution.py:748
  1.2 1.5 %collective-permute-start.1 = (f32[64,256]{1,0:T(8,128)}, f32[64,256]{1,0:T(8,128)S(1)}, u32[]{:S(2)}, u32[]{:S(2)}) collective-permute-start(f32[64,256]{1,0:T(8,128)} %bitcast.19), channel_id=1, source_target_pairs={{0,1},{1,0},{2,3},{3,2},{4,5},{5,4},{6,7},{7,6},{8,9},{9,8},{10,11... | collective-permute-start | bytes 196616 | tf_op jit(solution)/shard_map/ppermute | solution.py:748
  3.5 20.6 %all-to-all-start = ((f32[8,112,128]{2,1,0:T(8,128)}), f32[8,112,128]{2,1,0:T(8,128)S(1)}, u32[]{:S(2)}, u32[]{:S(2)}) async-start(f32[8,112,128]{2,1,0:T(8,128)} %bitcast.15), calls=%async_computation | async-start | bytes 917504 | tf_op jit(solution)/shard_map/all_to_all | solution.py:770
  32.5 11.0 %all-to-all-start.1 = ((f32[8,2,8,256]{3,2,1,0:T(8,128)}), f32[8,2,8,256]{3,2,1,0:T(8,128)S(1)}, u32[]{:S(2)}, u32[]{:S(2)}) async-start(f32[8,2,8,256]{3,2,1,0:T(8,128)} %get-tuple-element.15), calls=%async_computation.1 | async-start | bytes 262144 | tf_op jit(solution)/shard_map/all_to_all | solution.py:824

commit v4 on v3

--- a/solution.py
+++ b/solution.py
@@ -192,6 +192,7 @@
 LANES = 128
 SUBLANES = 8
 GROUP = 16
+UNROLL = 1
 SPAN = 2 * SEARCH + 1
 WINDOW = 2 * RADIUS + 1
 LOG2E = 1.4426950408889634
@@ -393,50 +394,38 @@
         running[s + 1] = total
 
 
-def invert(count, group, fresh, observed, inverse, lengths, plan, sparse, spread, running, steps):
+def invert_round(count, fresh, observed, inverse, lengths, plan, sparse, spread, running, steps):
+    groups = len(running)
     segments = 2 * count - 1
     threshold = SPARSITY / PENALTY
-    residual = [observed[pl.ds(group * SUBLANES * SUBLANES + j, SUBLANES, stride=SUBLANES), :] for j in range(count)]
-    if not fresh:
-        prefix(lengths, [spread[s] for s in range(segments)], running)
-        residual = [
-            residual[j] - (running[plan[count + j]] - running[plan[j]]) for j in range(count)
-        ]
-    for a in range(count):
-        step = inverse[a * count] * residual[0]
-        for b in range(1, count):
-            step = step + inverse[a * count + b] * residual[b]
-        steps[a] = step
-        steps[count + a] = -step
-    level = None
-    for s in range(segments):
-        rise = steps[plan[2 * count + s]]
-        level = rise if level is None else level + rise
-        blended = level if fresh else sparse[s + 1] + level
-        scaled = jnp.clip(blended, -threshold, threshold)
-        shrunk = blended - scaled
-        sparse[s + 1] = shrunk
-        spread[s] = shrunk - scaled
-
-
-def invert_round(count, fresh, observed, inverse, lengths, plan, sparse, spread, running, steps):
-    groups = len(running)
 
     def iterate(first):
+        if not first:
+            for group in range(groups):
+                prefix(lengths, [spread[group, s] for s in range(segments)], running[group])
         for group in range(groups):
-            invert(
-                count,
-                group,
-                first,
-                observed,
-                inverse,
-                lengths,
-                plan,
-                sparse.at[group],
-                spread.at[group],
-                running[group],
-                steps[group],
-            )
+            residual = []
+            for j in range(count):
+                value = observed[pl.ds(group * SUBLANES * SUBLANES + j, SUBLANES, stride=SUBLANES), :]
+                if not first:
+                    value = value - (running[group][plan[count + j]] - running[group][plan[j]])
+                residual.append(value)
+            for a in range(count):
+                terms = [inverse[a * count + b] * residual[b] for b in range(count)]
+                while len(terms) > 1:
+                    terms = [sum(terms[k : k + 2][1:], terms[k]) for k in range(0, len(terms), 2)]
+                steps[group][a] = terms[0]
+                steps[group][count + a] = -terms[0]
+        for group in range(groups):
+            level = None
+            for s in range(segments):
+                rise = steps[group][plan[2 * count + s]]
+                level = rise if level is None else level + rise
+                blended = level if first else sparse[group, s + 1] + level
+                scaled = jnp.clip(blended, -threshold, threshold)
+                shrunk = blended - scaled
+                sparse[group, s + 1] = shrunk
+                spread[group, s] = shrunk - scaled
 
     if fresh:
         iterate(True)
@@ -445,7 +434,7 @@
         iterate(False)
         return carry
 
-    lax.fori_loop(1 if fresh else 0, ITERS, later, 0, unroll=True)
+    lax.fori_loop(1 if fresh else 0, ITERS, later, 0, unroll=UNROLL)
 
 
 def velocity_kernel(matched, sparse_in, spread_in, inverse, lengths, plan, velocity, sparse, spread, *buffers):
@@ -527,7 +516,7 @@
             matched[pl.ds(at, SUBLANES), :] = value * share
         return carry
 
-    lax.fori_loop(0, cells, pixel_tile, 0, unroll=2)
+    lax.fori_loop(0, cells, pixel_tile, 0, unroll=4)
 
 
 def track_kernel(

time: 44.4 us -> 44.2 us (level)
  no operation moved by 1% of the time
where the time goes in v4:
time: 44.2 us; the launch traced here: 43.9 us
  Pallas kernels  16.3 us (37%)
  waiting for transfers between devices  14.9 us (34%)
  starting transfers between devices  11.2 us (25%)
  local copies, waits for them, and re-layouts  0.85 us (2%)
  between operations  0.69 us (2%)
    all_to_all x1, waiting for transfers between devices, by_strips(): lax.all_to_all(packed, 'pairs', split_axis=0, concat_axis=0, tiled=True)  10.5 us
    pallas_call x1, Pallas kernels, by_strips(): pl.pallas_call(track_kernel, out_shape=(jax.ShapeDtypeStruct((count, 2, s...  8.22 us
    all_to_all x1, starting transfers between devices, by_strips(): lax.all_to_all(packed, 'pairs', split_axis=0, concat_axis=0, tiled=True)  6.96 us
    all_to_all x1, waiting for transfers between devices, by_strips(): lax.all_to_all(motion, 'pairs', split_axis=0, concat_axis=0, tiled=True)  3.96 us
    all_to_all x1, starting transfers between devices, by_strips(): lax.all_to_all(motion, 'pairs', split_axis=0, concat_axis=0, tiled=True)  3.63 us
    pallas_call x1, Pallas kernels, by_strips(): pl.pallas_call(velocity_kernel, out_shape=jax.ShapeDtypeStruct((2, EPOCHS...  3.39 us
    pallas_call x1, Pallas kernels, by_strips(): pl.pallas_call(plan_kernel, out_shape=(shape(count * count), shape(segmen...  2.88 us
    pallas_call x1, Pallas kernels, by_strips(): pl.pallas_call(pack_kernel, out_shape=pltpu.VMEM(message, jnp.float32), i...  1.01 us
  transfers between devices with their start and end apart: 4, of which 3 were waited for; matrix products, arithmetic and copies ran while one was open for 0% of the time, Pallas kernels for 17%

profile of v4, /device:TPU:0, one launch (start us, length us, event | category | flops | bytes accessed | tf_op | source)
XLA Modules:
  0.0 43.9 jit_solution(9480757562128345824)
XLA Ops:
  0.6 0.0 copy-start.1
  0.6 0.0 copy-start.2
  0.7 0.0 copy-start
  0.7 0.6 %collective-permute-start = (f32[64,256]{1,0:T(8,128)}, f32[64,256]{1,0:T(8,128)S(1)}, u32[]{:S(2)}, u32[]{:S(2)}) collective-permute-start(f32[64,256]{1,0:T(8,128)} %bitcast.17), channel_id=1, source_target_pairs={{0,1},{1,0},{2,3},{3,2},{4,5},{5,4},{6,7},{7,6},{8,9},{9,8},{10,11... | collective-permute-start | bytes 196616 | tf_op jit(solution)/shard_map/ppermute | solution.py:737
  1.2 0.1 collective-permute-start.1
  1.3 1.0 %shard_map.77.packed = f32[896,128]{1,0:T(8,128)S(1)} custom-call(f32[64,256]{1,0:T(8,128)} %bitcast.18, f32[64,256]{1,0:T(8,128)} %bitcast.20, f32[2,64,256]{2,1,0:T(8,128)} %bitcast.16), custom_call_target="tpu_custom_call" | custom-call | tf_op jit(solution)/shard_map/pallas_call | solution.py:740
  2.3 0.0 collective-permute-done.other_first
  2.3 0.4 collective-permute-done.1.other_second
  2.7 0.8 %shard_map.78 = f32[896,128]{1,0:T(8,128)} custom-call(f32[64,256]{1,0:T(8,128)S(1)} %collective-permute-done.other_first, f32[64,256]{1,0:T(8,128)S(1)} %collective-permute-done.1.other_second, f32[896,128]{1,0:T(8,128)S(1)} %shard_map.77.packed), custom_call_target="tpu_custom_call" | custom-call | tf_op jit(solution)/shard_map/pallas_call | solution.py:748
  3.5 7.0 %all-to-all-start = ((f32[8,112,128]{2,1,0:T(8,128)}), f32[8,112,128]{2,1,0:T(8,128)S(1)}, u32[]{:S(2)}, u32[]{:S(2)}) async-start(f32[8,112,128]{2,1,0:T(8,128)} %bitcast.15), calls=%async_computation | async-start | bytes 917504 | tf_op jit(solution)/shard_map/all_to_all | solution.py:759
  10.4 0.0 copy-done.1
  10.4 0.1 copy.13.pair_epochs
  10.5 0.0 copy-done.2
  10.5 0.1 copy.14.offsets
  10.6 0.0 copy-done
  10.6 2.9 %shard_map.79 = (f32[64,8,128]{2,1,0:T(8,128)S(1)}, f32[15,8,128]{2,1,0:T(8,128)S(1)}, s32[146]{0:T(256)S(1)}) custom-call(s32[64,2]{1,0:T(8,128)S(1)} %copy.14.offsets, s32[8,2]{1,0:T(8,128)S(1)} %copy.13.pair_epochs, s32[8]{0:T(128)S(1)} %copy-done), custom_call_target="tpu_custom_call" | custom-call | tf_op jit(solution)/shard_map/pallas_call | solution.py:769
  13.5 10.5 %all-to-all-done = f32[8,112,128]{2,1,0:T(8,128)S(1)} async-done(((f32[8,112,128]{2,1,0:T(8,128)}), f32[8,112,128]{2,1,0:T(8,128)S(1)}, u32[]{:S(2)}, u32[]{:S(2)}) %all-to-all-start) | async-done | bytes 458784 | tf_op jit(solution)/shard_map/all_to_all | solution.py:759
  24.0 8.2 %shard_map.80 = (f32[8,2,8,256]{3,2,1,0:T(8,128)}, f32[256,128]{1,0:T(8,128)S(1)}, f32[4,17,8,128]{3,2,1,0:T(8,128)S(1)}, f32[4,15,8,128]{3,2,1,0:T(8,128)S(1)}) custom-call(s32[64,2]{1,0:T(8,128)S(1)} %copy.14.offsets, f32[896,128]{1,0:T(8,128)S(1)} %bitcast.13, f32[64,8,128]{2,1,0:T(8,128)S(1)} %get-tuple-element.9.inverse, ...), custom_call_target="tpu_custom_call" | custom-call | tf_op jit(solution)/shard_map/pallas_call | solution.py:780
  32.3 3.6 %all-to-all-start.1 = ((f32[8,2,8,256]{3,2,1,0:T(8,128)}), f32[8,2,8,256]{3,2,1,0:T(8,128)S(1)}, u32[]{:S(2)}, u32[]{:S(2)}) async-start(f32[8,2,8,256]{3,2,1,0:T(8,128)} %get-tuple-element.15), calls=%async_computation.1 | async-start | bytes 262144 | tf_op jit(solution)/shard_map/all_to_all | solution.py:813
  35.9 3.4 %shard_map.81 = f32[2,128,16,128]{3,2,1,0:T(8,128)} custom-call(f32[256,128]{1,0:T(8,128)S(1)} %get-tuple-element.12.matched, f32[4,17,8,128]{3,2,1,0:T(8,128)S(1)} %get-tuple-element.13.sparse_in, f32[4,15,8,128]{3,2,1,0:T(8,128)S(1)} %get-tuple-element.14.spread_in, f32[64,8,128]{2,1,0:T(8,128)S(1)} %get-tuple-element.9.inverse, ...), custom_call_target="tpu_custom_call" | custom-call | tf_op jit(solution)/shard_map/pallas_call | solution.py:805
  39.3 4.0 %all-to-all-done.1 = f32[8,2,8,256]{3,2,1,0:T(8,128)S(1)} async-done(((f32[8,2,8,256]{3,2,1,0:T(8,128)}), f32[8,2,8,256]{3,2,1,0:T(8,128)S(1)}, u32[]{:S(2)}, u32[]{:S(2)}) %all-to-all-start.1) | async-done | bytes 131104 | tf_op jit(solution)/shard_map/all_to_all | solution.py:813
  43.2 0.7 %copy_bitcast_fusion = f32[2,1,64,256]{3,2,1,0:T(8,128)} fusion(f32[8,2,8,256]{3,2,1,0:T(8,128)S(1)} %all-to-all-done.1), kind=kLoop, calls=%fused_computation | loop fusion | bytes 262144
Async XLA Ops:
  0.6 9.8 %copy-start.1 = (s32[8,2]{0,1:T(2,128)S(1)}, s32[8,2]{0,1:T(2,128)}, u32[]{:S(2)}) copy-start(s32[8,2]{0,1:T(2,128)} %param.10) | copy-start | bytes 196
  0.6 9.9 %copy-start.2 = (s32[64,2]{0,1:T(2,128)S(1)}, s32[64,2]{0,1:T(2,128)}, u32[]{:S(2)}) copy-start(s32[64,2]{0,1:T(2,128)} %param.9) | copy-start | bytes 1540
  0.7 10.0 %copy-start = (s32[8]{0:T(128)S(1)}, s32[8]{0:T(128)}, u32[]{:S(2)}) copy-start(s32[8]{0:T(128)} %pair_slot.1) | copy-start | bytes 100
  0.7 1.7 %collective-permute-start = (f32[64,256]{1,0:T(8,128)}, f32[64,256]{1,0:T(8,128)S(1)}, u32[]{:S(2)}, u32[]{:S(2)}) collective-permute-start(f32[64,256]{1,0:T(8,128)} %bitcast.17), channel_id=1, source_target_pairs={{0,1},{1,0},{2,3},{3,2},{4,5},{5,4},{6,7},{7,6},{8,9},{9,8},{10,11... | collective-permute-start | bytes 196616 | tf_op jit(solution)/shard_map/ppermute | solution.py:737
  1.2 1.5 %collective-permute-start.1 = (f32[64,256]{1,0:T(8,128)}, f32[64,256]{1,0:T(8,128)S(1)}, u32[]{:S(2)}, u32[]{:S(2)}) collective-permute-start(f32[64,256]{1,0:T(8,128)} %bitcast.19), channel_id=1, source_target_pairs={{0,1},{1,0},{2,3},{3,2},{4,5},{5,4},{6,7},{7,6},{8,9},{9,8},{10,11... | collective-permute-start | bytes 196616 | tf_op jit(solution)/shard_map/ppermute | solution.py:737
  3.5 20.6 %all-to-all-start = ((f32[8,112,128]{2,1,0:T(8,128)}), f32[8,112,128]{2,1,0:T(8,128)S(1)}, u32[]{:S(2)}, u32[]{:S(2)}) async-start(f32[8,112,128]{2,1,0:T(8,128)} %bitcast.15), calls=%async_computation | async-start | bytes 917504 | tf_op jit(solution)/shard_map/all_to_all | solution.py:759
  32.3 11.0 %all-to-all-start.1 = ((f32[8,2,8,256]{3,2,1,0:T(8,128)}), f32[8,2,8,256]{3,2,1,0:T(8,128)S(1)}, u32[]{:S(2)}, u32[]{:S(2)}) async-start(f32[8,2,8,256]{3,2,1,0:T(8,128)} %get-tuple-element.15), calls=%async_computation.1 | async-start | bytes 262144 | tf_op jit(solution)/shard_map/all_to_all | solution.py:813

commit v5 on v4

--- a/solution.py
+++ b/solution.py
@@ -564,7 +564,8 @@
             table[at + cell] = nothing
         return carry
 
-    lax.fori_loop(0, SPAN * SPAN - offsets.shape[0], clear, 0)
+    for index in range(SPAN * SPAN - offsets.shape[0]):
+        clear(index, 0)
 
     tap = lax.broadcasted_iota(jnp.int32, band.shape[1:], 0)
     column = lax.broadcasted_iota(jnp.int32, band.shape[1:], 1)

time: 44.2 us -> 44.1 us (level)
  no operation moved by 1% of the time
where the time goes in v5:
time: 44.1 us; the launch traced here: 43.7 us
  Pallas kernels  16.1 us (37%)
  waiting for transfers between devices  14.9 us (34%)
  starting transfers between devices  11.2 us (25%)
  local copies, waits for them, and re-layouts  0.85 us (2%)
  between operations  0.69 us (2%)
    all_to_all x1, waiting for transfers between devices, by_strips(): lax.all_to_all(packed, 'pairs', split_axis=0, concat_axis=0, tiled=True)  10.5 us
    pallas_call x1, Pallas kernels, by_strips(): pl.pallas_call(track_kernel, out_shape=(jax.ShapeDtypeStruct((count, 2, s...  8.07 us
    all_to_all x1, starting transfers between devices, by_strips(): lax.all_to_all(packed, 'pairs', split_axis=0, concat_axis=0, tiled=True)  6.96 us
    all_to_all x1, waiting for transfers between devices, by_strips(): lax.all_to_all(motion, 'pairs', split_axis=0, concat_axis=0, tiled=True)  3.97 us
    all_to_all x1, starting transfers between devices, by_strips(): lax.all_to_all(motion, 'pairs', split_axis=0, concat_axis=0, tiled=True)  3.64 us
    pallas_call x1, Pallas kernels, by_strips(): pl.pallas_call(velocity_kernel, out_shape=jax.ShapeDtypeStruct((2, EPOCHS...  3.38 us
    pallas_call x1, Pallas kernels, by_strips(): pl.pallas_call(plan_kernel, out_shape=(shape(count * count), shape(segmen...  2.88 us
    pallas_call x1, Pallas kernels, by_strips(): pl.pallas_call(pack_kernel, out_shape=pltpu.VMEM(message, jnp.float32), i...  1.01 us
  transfers between devices with their start and end apart: 4, of which 3 were waited for; matrix products, arithmetic and copies ran while one was open for 0% of the time, Pallas kernels for 17%

profile of v5, /device:TPU:0, one launch (start us, length us, event | category | flops | bytes accessed | tf_op | source)
XLA Modules:
  0.0 43.7 jit_solution(8772926892647119450)
XLA Ops:
  0.6 0.0 copy-start.1
  0.6 0.0 copy-start.2
  0.7 0.0 copy-start
  0.7 0.6 %collective-permute-start = (f32[64,256]{1,0:T(8,128)}, f32[64,256]{1,0:T(8,128)S(1)}, u32[]{:S(2)}, u32[]{:S(2)}) collective-permute-start(f32[64,256]{1,0:T(8,128)} %bitcast.17), channel_id=1, source_target_pairs={{0,1},{1,0},{2,3},{3,2},{4,5},{5,4},{6,7},{7,6},{8,9},{9,8},{10,11... | collective-permute-start | bytes 196616 | tf_op jit(solution)/shard_map/ppermute | solution.py:738
  1.2 0.1 collective-permute-start.1
  1.3 1.0 %shard_map.77.packed = f32[896,128]{1,0:T(8,128)S(1)} custom-call(f32[64,256]{1,0:T(8,128)} %bitcast.18, f32[64,256]{1,0:T(8,128)} %bitcast.20, f32[2,64,256]{2,1,0:T(8,128)} %bitcast.16), custom_call_target="tpu_custom_call" | custom-call | tf_op jit(solution)/shard_map/pallas_call | solution.py:741
  2.3 0.0 collective-permute-done.other_first
  2.3 0.4 collective-permute-done.1.other_second
  2.7 0.8 %shard_map.78 = f32[896,128]{1,0:T(8,128)} custom-call(f32[64,256]{1,0:T(8,128)S(1)} %collective-permute-done.other_first, f32[64,256]{1,0:T(8,128)S(1)} %collective-permute-done.1.other_second, f32[896,128]{1,0:T(8,128)S(1)} %shard_map.77.packed), custom_call_target="tpu_custom_call" | custom-call | tf_op jit(solution)/shard_map/pallas_call | solution.py:749
  3.5 7.0 %all-to-all-start = ((f32[8,112,128]{2,1,0:T(8,128)}), f32[8,112,128]{2,1,0:T(8,128)S(1)}, u32[]{:S(2)}, u32[]{:S(2)}) async-start(f32[8,112,128]{2,1,0:T(8,128)} %bitcast.15), calls=%async_computation | async-start | bytes 917504 | tf_op jit(solution)/shard_map/all_to_all | solution.py:760
  10.4 0.0 copy-done.1
  10.4 0.1 copy.13.pair_epochs
  10.5 0.0 copy-done.2
  10.5 0.1 copy.14.offsets
  10.6 0.0 copy-done
  10.6 2.9 %shard_map.79 = (f32[64,8,128]{2,1,0:T(8,128)S(1)}, f32[15,8,128]{2,1,0:T(8,128)S(1)}, s32[146]{0:T(256)S(1)}) custom-call(s32[64,2]{1,0:T(8,128)S(1)} %copy.14.offsets, s32[8,2]{1,0:T(8,128)S(1)} %copy.13.pair_epochs, s32[8]{0:T(128)S(1)} %copy-done), custom_call_target="tpu_custom_call" | custom-call | tf_op jit(solution)/shard_map/pallas_call | solution.py:770
  13.5 10.5 %all-to-all-done = f32[8,112,128]{2,1,0:T(8,128)S(1)} async-done(((f32[8,112,128]{2,1,0:T(8,128)}), f32[8,112,128]{2,1,0:T(8,128)S(1)}, u32[]{:S(2)}, u32[]{:S(2)}) %all-to-all-start) | async-done | bytes 458784 | tf_op jit(solution)/shard_map/all_to_all | solution.py:760
  24.0 8.1 %shard_map.80 = (f32[8,2,8,256]{3,2,1,0:T(8,128)}, f32[256,128]{1,0:T(8,128)S(1)}, f32[4,17,8,128]{3,2,1,0:T(8,128)S(1)}, f32[4,15,8,128]{3,2,1,0:T(8,128)S(1)}) custom-call(s32[64,2]{1,0:T(8,128)S(1)} %copy.14.offsets, f32[896,128]{1,0:T(8,128)S(1)} %bitcast.13, f32[64,8,128]{2,1,0:T(8,128)S(1)} %get-tuple-element.9.inverse, ...), custom_call_target="tpu_custom_call" | custom-call | tf_op jit(solution)/shard_map/pallas_call | solution.py:781
  32.1 3.6 %all-to-all-start.1 = ((f32[8,2,8,256]{3,2,1,0:T(8,128)}), f32[8,2,8,256]{3,2,1,0:T(8,128)S(1)}, u32[]{:S(2)}, u32[]{:S(2)}) async-start(f32[8,2,8,256]{3,2,1,0:T(8,128)} %get-tuple-element.15), calls=%async_computation.1 | async-start | bytes 262144 | tf_op jit(solution)/shard_map/all_to_all | solution.py:814
  35.7 3.4 %shard_map.81 = f32[2,128,16,128]{3,2,1,0:T(8,128)} custom-call(f32[256,128]{1,0:T(8,128)S(1)} %get-tuple-element.12.matched, f32[4,17,8,128]{3,2,1,0:T(8,128)S(1)} %get-tuple-element.13.sparse_in, f32[4,15,8,128]{3,2,1,0:T(8,128)S(1)} %get-tuple-element.14.spread_in, f32[64,8,128]{2,1,0:T(8,128)S(1)} %get-tuple-element.9.inverse, ...), custom_call_target="tpu_custom_call" | custom-call | tf_op jit(solution)/shard_map/pallas_call | solution.py:806
  39.1 4.0 %all-to-all-done.1 = f32[8,2,8,256]{3,2,1,0:T(8,128)S(1)} async-done(((f32[8,2,8,256]{3,2,1,0:T(8,128)}), f32[8,2,8,256]{3,2,1,0:T(8,128)S(1)}, u32[]{:S(2)}, u32[]{:S(2)}) %all-to-all-start.1) | async-done | bytes 131104 | tf_op jit(solution)/shard_map/all_to_all | solution.py:814
  43.1 0.7 %copy_bitcast_fusion = f32[2,1,64,256]{3,2,1,0:T(8,128)} fusion(f32[8,2,8,256]{3,2,1,0:T(8,128)S(1)} %all-to-all-done.1), kind=kLoop, calls=%fused_computation | loop fusion | bytes 262144
Async XLA Ops:
  0.6 9.8 %copy-start.1 = (s32[8,2]{0,1:T(2,128)S(1)}, s32[8,2]{0,1:T(2,128)}, u32[]{:S(2)}) copy-start(s32[8,2]{0,1:T(2,128)} %param.10) | copy-start | bytes 196
  0.6 9.9 %copy-start.2 = (s32[64,2]{0,1:T(2,128)S(1)}, s32[64,2]{0,1:T(2,128)}, u32[]{:S(2)}) copy-start(s32[64,2]{0,1:T(2,128)} %param.9) | copy-start | bytes 1540
  0.7 10.0 %copy-start = (s32[8]{0:T(128)S(1)}, s32[8]{0:T(128)}, u32[]{:S(2)}) copy-start(s32[8]{0:T(128)} %pair_slot.1) | copy-start | bytes 100
  0.7 1.7 %collective-permute-start = (f32[64,256]{1,0:T(8,128)}, f32[64,256]{1,0:T(8,128)S(1)}, u32[]{:S(2)}, u32[]{:S(2)}) collective-permute-start(f32[64,256]{1,0:T(8,128)} %bitcast.17), channel_id=1, source_target_pairs={{0,1},{1,0},{2,3},{3,2},{4,5},{5,4},{6,7},{7,6},{8,9},{9,8},{10,11... | collective-permute-start | bytes 196616 | tf_op jit(solution)/shard_map/ppermute | solution.py:738
  1.2 1.5 %collective-permute-start.1 = (f32[64,256]{1,0:T(8,128)}, f32[64,256]{1,0:T(8,128)S(1)}, u32[]{:S(2)}, u32[]{:S(2)}) collective-permute-start(f32[64,256]{1,0:T(8,128)} %bitcast.19), channel_id=1, source_target_pairs={{0,1},{1,0},{2,3},{3,2},{4,5},{5,4},{6,7},{7,6},{8,9},{9,8},{10,11... | collective-permute-start | bytes 196616 | tf_op jit(solution)/shard_map/ppermute | solution.py:738
  3.5 20.6 %all-to-all-start = ((f32[8,112,128]{2,1,0:T(8,128)}), f32[8,112,128]{2,1,0:T(8,128)S(1)}, u32[]{:S(2)}, u32[]{:S(2)}) async-start(f32[8,112,128]{2,1,0:T(8,128)} %bitcast.15), calls=%async_computation | async-start | bytes 917504 | tf_op jit(solution)/shard_map/all_to_all | solution.py:760
  32.1 11.0 %all-to-all-start.1 = ((f32[8,2,8,256]{3,2,1,0:T(8,128)}), f32[8,2,8,256]{3,2,1,0:T(8,128)S(1)}, u32[]{:S(2)}, u32[]{:S(2)}) async-start(f32[8,2,8,256]{3,2,1,0:T(8,128)} %get-tuple-element.15), calls=%async_computation.1 | async-start | bytes 262144 | tf_op jit(solution)/shard_map/all_to_all | solution.py:814
